TPU v7x, 32 devices: a whole 2x2x4 slice. The times are simulated.
32 devices in a mesh: dp: 8 (over z, x), tensor: 4 (over y, core).
Axes of the slice: x: 2, y: 2, z: 4, core: 2. Of those that a mesh axis runs over, the one named last changes fastest.
Arguments:
- hidden_in: bfloat16 [16, 1024, 1024], P('dp', 'tensor'), may hold values from -6 to 6
- out_grad: bfloat16 [16, 1024, 1024], P('dp', 'tensor'), may hold values from -6 to 6
- doc_ids: int32 [16, 1, 1024], P('dp'), may hold values from 0 to 2, never falling along the last dimension, each value on 1 to 512 neighbouring positions
- w_query: bfloat16 [1024, 1024], P('dp', 'tensor'), may hold values from -0.1875 to 0.1875
- w_key: bfloat16 [1024, 1024], P('dp', 'tensor'), may hold values from -0.1875 to 0.1875
- w_value: bfloat16 [1024, 1024], P('dp', 'tensor'), may hold values from -0.1875 to 0.1875
- w_output: bfloat16 [1024, 1024], P('tensor', 'dp'), may hold values from -0.1875 to 0.1875
- w_up: bfloat16 [1024, 4096], P('dp', 'tensor'), may hold values from -0.1875 to 0.1875
- w_gate: bfloat16 [1024, 4096], P('dp', 'tensor'), may hold values from -0.1875 to 0.1875
- w_down: bfloat16 [4096, 1024], P('tensor', 'dp'), may hold values from -0.09375 to 0.09375
- scale_qk: float32 [1024], P(('dp', 'tensor')), may hold values from 0.8 to 1.6
- alpha_attn: float32 [1024], P(('dp', 'tensor')), may hold values from 0.2 to 0.8
- alpha_mlp: float32 [1024], P(('dp', 'tensor')), may hold values from 0.2 to 0.8
- scale_up: float32 [4096], P(('dp', 'tensor')), may hold values from 0.5 to 2
- scale_gate: float32 [4096], P(('dp', 'tensor')), may hold values from 0.5 to 2
Outputs:
- layer_out: bfloat16 [16, 1024, 1024], P('dp', 'tensor')
- input_grad: bfloat16 [16, 1024, 1024], P('dp', 'tensor')
- grad_query: float32 [1024, 1024], P('dp', 'tensor')
- grad_key: float32 [1024, 1024], P('dp', 'tensor')
- grad_value: float32 [1024, 1024], P('dp', 'tensor')
- grad_output: float32 [1024, 1024], P('tensor', 'dp')
- grad_up: float32 [1024, 4096], P('dp', 'tensor')
- grad_gate: float32 [1024, 4096], P('dp', 'tensor')
- grad_down: float32 [4096, 1024], P('tensor', 'dp')
- grad_scale_qk: float32 [1024], P(('dp', 'tensor'))
- grad_alpha_attn: float32 [1024], P(('dp', 'tensor'))
- grad_alpha_mlp: float32 [1024], P(('dp', 'tensor'))
- grad_scale_up: float32 [4096], P(('dp', 'tensor'))
- grad_scale_gate: float32 [4096], P(('dp', 'tensor'))
Inputs may be any that keep to these rules, and one draw needn't show every extreme that they name: `doc_ids`: each sequence packs 3 documents of ids 0 to 2 in order, each of at most 512 tokens.
All inputs are finite; a program needn't handle non-finite values.
Results may differ from a plain program's by a relative error of at most 0.028.
Values may be sent and summed in bfloat16 or wider, within the bound.
A program may use at most 192 MiB of HBM per device.

v0:
```python
import functools
import math

import jax
import jax.numpy as jnp
from jax import lax
from jax.experimental import pallas as pl
from jax.experimental.pallas import tpu as pltpu
from jax.sharding import PartitionSpec as P

DH = 64
BLOCK = 256
DOCS = 3
DOC_MAX = 512
F32 = jnp.float32
BF16 = jnp.bfloat16
MESH = pl.DeviceIdType.MESH
VMEM_LIMIT = 67043328
LOG2E = 1.4426950408889634
QB = 128
COLS = 256
CODE = 8


def nn(a, b):
    return jnp.dot(a, b, preferred_element_type=F32)


def nt(a, b):
    return lax.dot_general(a, b, (((1,), (1,)), ((), ())), preferred_element_type=F32)


def tn(a, b):
    return lax.dot_general(a, b, (((0,), (0,)), ((), ())), preferred_element_type=F32)


def split_sum(vals, ones):
    high = vals.astype(BF16)
    low = (vals - high.astype(F32)).astype(BF16)
    return nn(high, ones) + nn(low, ones)


def lane_iota(shape):
    return lax.broadcasted_iota(jnp.int32, shape, len(shape) - 1)


def head_ones():
    rows = lax.broadcasted_iota(jnp.int32, (128, 128), 0) // DH
    cols = lax.broadcasted_iota(jnp.int32, (128, 128), 1) // DH
    return jnp.where(rows == cols, 1.0, 0.0).astype(BF16)


def partner(vals):
    low = lane_iota(vals.shape) % DH < DH // 2
    return jnp.where(low, pltpu.roll(vals, 128 - DH // 2, 1), pltpu.roll(vals, DH // 2, 1))


def turns(table):
    lane = lane_iota(table.shape)
    both = jnp.where(lane < DH, table, pltpu.roll(table, DH, 1))
    low = lane % DH < DH // 2
    cosine = jnp.where(low, both, pltpu.roll(both, DH // 2, 1))
    sine = jnp.where(low, -pltpu.roll(both, 128 - DH // 2, 1), both)
    return cosine, sine


class Place:
    def __init__(self, n):
        self.n = n
        self.t = lax.axis_index("tensor")
        self.d = lax.axis_index("dp")
        t, d = self.t, self.d
        self.sib = t + 1 - 2 * (t % 2)
        self.yp = (t + 2) % 4
        self.diag = (self.sib + 2) % 4
        self.xi = d % 2
        self.z = d // 2
        self.nz = n // 2
        self.xn = d + 1 - 2 * (d % 2)
        self.zpeers = [2 * ((self.z + k) % self.nz) + self.xi for k in range(1, self.nz)]
        self.dpeers = [(d + k) % n for k in range(1, n)]
        self.tpeers = [(t + k) % 4 for k in range(1, 4)]

    def barrier(self):
        sem = pltpu.get_barrier_semaphore()
        for peer in self.dpeers:
            pl.semaphore_signal(sem, inc=1, device_id={"dp": peer}, device_id_type=MESH)
        for peer in self.tpeers:
            pl.semaphore_signal(sem, inc=1, device_id={"tensor": peer}, device_id_type=MESH)
        pl.semaphore_wait(sem, self.n + 2)


def remote(src, dst, ssem, rsem, **where):
    return pltpu.make_async_remote_copy(
        src_ref=src, dst_ref=dst, send_sem=ssem, recv_sem=rsem, device_id=where, device_id_type=MESH
    )


class Gather:
    def __init__(self, place, whole, ssem, rsem, rows):
        self.p, self.whole, self.ssem, self.rsem, self.rows = place, whole, ssem, rsem, rows

    def at(self, index):
        return self.whole.at[pl.ds(pl.multiple_of(index * self.rows, self.rows), self.rows)]

    def start(self, own):
        p = self.p
        self.c_yp = remote(own, self.at(p.t), self.ssem.at[1], self.rsem.at[1], tensor=p.yp)
        self.c_sib = remote(own, self.at(p.t), self.ssem.at[0], self.rsem.at[0], tensor=p.sib)
        self.c_yp.start()
        self.c_sib.start()

    def wait(self, step):
        p = self.p
        if step == 1:
            remote(self.at(p.sib), self.at(p.sib), self.ssem.at[0], self.rsem.at[0], tensor=p.sib).wait_recv()
        if step == 2:
            remote(self.at(p.yp), self.at(p.yp), self.ssem.at[1], self.rsem.at[1], tensor=p.yp).wait_recv()
            self.forward().start()
        if step == 3:
            remote(self.at(p.diag), self.at(p.diag), self.ssem.at[2], self.rsem.at[2], tensor=p.sib).wait_recv()

    def forward(self):
        p = self.p
        return remote(self.at(p.yp), self.at(p.yp), self.ssem.at[2], self.rsem.at[2], tensor=p.sib)

    def drain(self):
        self.c_yp.wait_send()
        self.c_sib.wait_send()
        self.forward().wait_send()

    def each(self, work):
        blocks(self.p, work, self.wait)


def blocks(p, work, wait=None):
    def body(i, carry):
        for step in range(1, 4):
            if wait is not None:
                pl.when(i == step)(functools.partial(wait, step))
        work((p.t // 2 + i // 2) % 2 * 2 + (p.t + i) % 2)
        return carry

    lax.fori_loop(0, 4, body, 0)


class Scatter:
    def __init__(self, place, sbuf, rbuf, ssem, rsem):
        self.p, self.sbuf, self.rbuf, self.ssem, self.rsem = place, sbuf, rbuf, ssem, rsem
        self.copies = []

    def send(self, slot, **where):
        copy = remote(
            self.sbuf.at[slot], self.rbuf.at[slot], self.ssem.at[slot], self.rsem.at[slot], **where
        )
        copy.start()
        self.copies.append(copy)

    def arrive(self, slot):
        remote(
            self.rbuf.at[slot], self.rbuf.at[slot], self.ssem.at[slot], self.rsem.at[slot],
            tensor=self.p.sib,
        ).wait_recv()

    def run(self, part, own):
        p = self.p
        width = own.shape[1]

        def fill(index, put):
            def body(c, carry):
                lanes = pl.ds(pl.multiple_of(c * COLS, COLS), COLS)
                put(lanes, part(index, lanes))
                return carry

            lax.fori_loop(0, width // COLS, body, 0)

        def first(slot):
            def put(lanes, vals):
                self.sbuf[slot, :, lanes] = vals.astype(BF16)

            return put

        def across(lanes, vals):
            self.sbuf[2, :, lanes] = (vals + self.rbuf[0, :, lanes].astype(F32)).astype(BF16)

        def mine(lanes, vals):
            own[:, lanes] = vals

        fill(p.diag, first(0))
        self.send(0, tensor=p.sib)
        fill(p.sib, first(1))
        self.send(1, tensor=p.sib)
        self.arrive(0)
        fill(p.yp, across)
        self.send(2, tensor=p.yp)
        fill(p.t, mine)

    def finish(self):
        self.arrive(1)
        self.arrive(2)
        for copy in self.copies:
            copy.wait_send()


def rows_of(ref, index, rows):
    return ref[pl.ds(pl.multiple_of(index * rows, rows), rows)]


def mean_sq(vals):
    return jnp.mean(vals * vals, axis=-1, keepdims=True)


def fold8(vals):
    total = vals[0:8]
    for k in range(1, vals.shape[0] // 8):
        total = total + vals[8 * k : 8 * k + 8]
    return total


def fwd_kernel(
    n,
    wq, wk, wv, wo, wu, wg, wd, hid, og, small, docs,
    o_out, o_w, o_x, o_q, o_k, o_v, o_rq, o_rk, o_lrow, o_mixed, o_mid, o_up, o_gate, o_inner,
    o_attn, o_gmd, o_gm, o_gm0, o_vec, o_acc, o_tab, o_ir,
    w, x, q, k, v, rq, rk, lcol, mixed, mid, up, gate, inner,
    attn, midf, mlp, gmd, gm, gm0, vec, acc, tab, ir, sall, docv, ogv, outv, qm, sbuf, rbuf,
    wsend, wrecv, small_s, small_r, lsem, agx_s, agx_r, agm_s, agm_r, agg_s, agg_r,
    rsa_s, rsa_r, rsm_s, rsm_r, osem,
):
    p = Place(n)
    nz = p.nz
    mbs, rows, width = hid.shape
    seq = x.shape[1]
    hw = q.shape[2]
    shard = wq.shape[0]
    heads = hw // DH
    groups = w.shape[0]
    hidden = up.shape[2]

    def wat(g, index):
        return w.at[g, pl.ds(pl.multiple_of(index * shard, shard), shard)]

    local = []

    def lcopy(src, dst):
        copy = pltpu.make_async_copy(src, dst, lsem.at[len(local)])
        copy.start()
        local.append(copy)
        return copy

    outs = []

    def ocopy(src, dst):
        copy = pltpu.make_async_copy(src, dst, osem.at[len(outs)])
        copy.start()
        outs.append(copy)

    own_w = pl.ds(pl.multiple_of(p.d * shard, shard), shard)
    w_in = [lcopy(src, w.at[0, own_w, pl.ds(i * hw, hw)]) for i, src in enumerate((wq, wk, wv, wo))]
    w_in += [lcopy(src, w.at[i + 1, own_w]) for i, src in enumerate((wu, wg, wd))]
    docs_in = lcopy(docs, docv)
    p.barrier()

    gx = [Gather(p, x.at[m], agx_s.at[m], agx_r.at[m], rows) for m in range(mbs)]
    gmi = [Gather(p, mid.at[m], agm_s.at[m], agm_r.at[m], rows) for m in range(mbs)]
    slot = p.t * n + p.d
    small_own = lcopy(small, sall.at[slot])
    small_d = [
        remote(small, sall.at[slot], small_s.at[i], small_r.at[i], dp=peer)
        for i, peer in enumerate(p.dpeers)
    ]
    for copy in small_d:
        copy.start()
    gx[0].start(hid.at[0])
    sends = []

    def wsend_to(g, i, src, index, peer):
        copy = remote(src, wat(g, index), wsend.at[g, i], wrecv.at[g, index], dp=peer)
        copy.start()
        sends.append(copy)

    def relay(g):
        for i, peer in reversed(list(enumerate(p.zpeers))):
            remote(wat(g, peer), wat(g, peer), wsend.at[g, 0], wrecv.at[g, peer], dp=p.xn).wait_recv()
            wsend_to(g, nz + i, wat(g, peer), peer, p.xn)

    for copy in w_in:
        copy.wait()
    for g in range(groups):
        for i, peer in enumerate(p.zpeers):
            wsend_to(g, i, wat(g, p.d), p.d, peer)
        if g == 0:
            wsend_to(0, nz - 1, wat(0, p.d), p.d, p.xn)
    xown = [lcopy(hid.at[m], gx[m].at(p.t)) for m in range(mbs)]
    og_in = lcopy(og, ogv)
    for i, peer in enumerate(p.dpeers):
        src = p.t * n + (p.d + n - (i + 1)) % n
        remote(sall.at[src], sall.at[src], small_s.at[i], small_r.at[i], dp=peer).wait_recv()
    small_own.wait()
    small_t = []
    for i, peer in enumerate(p.tpeers):
        part = sall.at[pl.ds(p.t * n, n)]
        copy = remote(part, part, small_s.at[n - 1 + i], small_r.at[n - 1 + i], tensor=peer)
        copy.start()
        small_t.append(copy)
    gx[1].start(hid.at[1])

    def wready(g):
        remote(wat(g, p.xn), wat(g, p.xn), wsend.at[g, 0], wrecv.at[g, p.xn], dp=p.xn).wait_recv()
        for peer in p.zpeers:
            other = peer + 1 - 2 * p.xi
            remote(wat(g, other), wat(g, other), wsend.at[g, 0], wrecv.at[g, other], dp=p.xn).wait_recv()
        ocopy(w.at[g], o_w.at[g])

    docs_in.wait()
    for m in range(mbs):
        doc = docv[m]
        count = [jnp.sum(jnp.where(doc == i, 1.0, 0.0), axis=1, keepdims=True) for i in range(DOCS - 1)]
        first = jnp.zeros(doc.shape, F32)
        for i in range(DOCS - 1):
            first = first + jnp.where(doc > i, count[i], 0.0)
        place = lane_iota(doc.shape).astype(F32) - first
        low = doc.astype(F32) * CODE
        code = low + jnp.floor(place * (1.0 / BLOCK))
        line = lax.broadcasted_iota(jnp.int32, (8, seq), 0)
        ir[m] = jnp.where(line == 0, code, jnp.where(line == 1, low, place))
        line = lax.broadcasted_iota(jnp.int32, (128, seq), 0)
        every_row = jnp.where(line == DH, code, jnp.where(line == DH + 1, low, place))
        tab[m] = jnp.transpose(every_row, (1, 0))

    def turn_rows(i, carry):
        at = pl.ds(pl.multiple_of(i % (seq // 64) * 64, 64), 64)
        m = i // (seq // 64)
        lane = lane_iota((1, 128))
        freq = jnp.exp((lane % (DH // 2)).astype(F32) * (-math.log(10000.0) / (DH // 2)))
        shift = jnp.where(lane < DH // 2, 0.5 * math.pi, 0.0)
        old = tab[m, at, :]
        tab[m, at, :] = jnp.where(lane < DH, jnp.sin(old[:, 0:1] * freq + shift), old)
        return carry

    lax.fori_loop(0, mbs * (seq // 64), turn_rows, 0)
    acc[...] = jnp.zeros_like(acc)

    relay(0)
    for g in range(1, groups):
        wsend_to(g, nz - 1, wat(g, p.d), p.d, p.xn)
    for i, peer in enumerate(p.tpeers):
        part = sall.at[pl.ds((p.t + 4 - (i + 1)) % 4 * n, n)]
        remote(part, part, small_s.at[n - 1 + i], small_r.at[n - 1 + i], tensor=peer).wait_recv()
    every = 4 * n

    def gathered(row, base, count, lanes):
        per = count // (lanes // 128)

        def item(k):
            part = sall[k % 4 * n + base + k // 4, row : row + 1, :]
            turn = k % per * (128 // per)
            return pltpu.roll(part, turn, 1) if turn else part

        for r in range(lanes // 128):
            total = item(r * per)
            for j in range(1, per):
                total = total + item(r * per + j)
            vec[row : row + 1, 128 * r : 128 * r + 128] = total

    gathered(0, p.t * (n // 4), n, hw)
    gathered(1, 0, every, width)
    gathered(2, 0, every, width)
    gathered(3, p.t * (n // 4), n, hidden)
    gathered(4, p.t * (n // 4), n, hidden)
    wready(0)

    ones = head_ones()

    def stage_qkv(m):
        xown[m].wait()

        def work(index):
            at = pl.ds(pl.multiple_of(index * rows, rows), rows)
            xb = x[m, at, :]
            cb, sb = turns(tab[m, at, :])
            for which, (dst, rdst) in enumerate(((q, rq), (k, rk))):
                raw = nn(xb, w[0, :, which * hw : (which + 1) * hw])
                for half in range(hw // 128):
                    lanes = slice(128 * half, 128 * half + 128)
                    piece = raw[:, lanes]
                    turned = piece * cb + partner(piece) * sb
                    scale = lax.rsqrt(split_sum(turned * turned, ones) + 1e-06)
                    rdst[m, at, lanes] = scale.astype(BF16)
                    dst[m, at, lanes] = (turned * scale * vec[0:1, lanes]).astype(BF16)
            v[m, at, :] = nn(xb, w[0, :, 2 * hw : 3 * hw]).astype(BF16)

        gx[m].each(work)

    win = seq - 128
    c_exp = math.sqrt(DH) * LOG2E

    def attend(m):
        def body(b, carry):
            at = pl.ds(pl.multiple_of(b * QB, QB), QB)
            keys = pl.ds(pl.multiple_of(((b + 3) // 8) * 128, 128), win)
            ccol = tab[m, at, DH : DH + 1]
            lcol_ = tab[m, at, DH + 1 : DH + 2]
            crow = ir[m, 0:1, keys]
            bias = jnp.where((crow <= ccol) & (crow >= lcol_), 0.0, -1e30)
            qb = q[m, at, :]
            lane = lane_iota((QB, hw)) // DH
            for h in range(heads):
                qm[h * QB : (h + 1) * QB, :] = jnp.where(lane == h, qb, jnp.zeros_like(qb))
            kb = k[m, keys, :]
            vb = v[m, keys, :]
            total = jnp.zeros((QB, hw), F32)
            lsum = jnp.zeros((QB, 128), F32)
            lane_l = lane_iota((QB, 128))
            for h in range(heads):
                scores = nt(qm[h * QB : (h + 1) * QB, :], kb)
                expo = jnp.exp2(scores * c_exp + bias)
                inv = 1.0 / jnp.sum(expo, axis=-1, keepdims=True)
                part = nn(expo.astype(BF16), vb)
                total = jnp.where(lane == h, part * inv, total)
                lsum = jnp.where(lane_l == h, inv, lsum)
            mixed[m, at, :] = total.astype(BF16)
            lcol[m, at, :] = lsum
            return carry

        lax.fori_loop(0, seq // QB, body, 0)

    sc_a = [Scatter(p, sbuf.at[m], rbuf.at[m], rsa_s.at[m], rsa_r.at[m]) for m in range(mbs)]
    sc_m = [Scatter(p, sbuf.at[m], rbuf.at[m], rsm_s.at[m], rsm_r.at[m]) for m in range(mbs)]

    def stage_o(m):
        sc_a[m].run(
            lambda index, cols: nt(rows_of(mixed.at[m], index, rows), w[0, cols, 3 * hw : 3 * hw + hw]),
            attn.at[m],
        )

    chunk = 32

    def stage_mid(m):
        sc_a[m].finish()
        base = p.t * rows

        def body(i, carry):
            at = pl.ds(pl.multiple_of(i * chunk, chunk), chunk)
            own = pl.ds(pl.multiple_of(base + i * chunk, chunk), chunk)
            a = attn[m, at, :] + rbuf[m, 1, at, :].astype(F32) + rbuf[m, 2, at, :].astype(F32)
            attn[m, at, :] = a
            h = x[m, own, :].astype(F32)
            na = a * lax.rsqrt(mean_sq(a) + 1e-06)
            zz = h + vec[1:2, :] * (na - h)
            out = zz * lax.rsqrt(mean_sq(zz) + 1e-06)
            midf[m, at, :] = out
            mid[m, own, :] = out.astype(BF16)
            return carry

        lax.fori_loop(0, rows // chunk, body, 0)
        gmi[m].start(gmi[m].at(p.t))

    cols = 256

    def stage_up(m):
        def work(index):
            at = pl.ds(pl.multiple_of(index * rows, rows), rows)

            def body(c, carry):
                lanes = pl.ds(pl.multiple_of(c * cols, cols), cols)
                mb = mid[m, at, :]
                u = nn(mb, w[1, :, lanes])
                g = nn(mb, w[2, :, lanes])
                up[m, at, lanes] = u.astype(BF16)
                gate[m, at, lanes] = g.astype(BF16)
                gs = g * vec[4:5, lanes]
                inner[m, at, lanes] = ((u * vec[3:4, lanes]) * (gs / (1.0 + jnp.exp(-gs)))).astype(BF16)
                return carry

            lax.fori_loop(0, hidden // cols, body, 0)

        gmi[m].each(work)

    def stage_down(m):
        sc_m[m].run(lambda index, cols: nt(rows_of(inner.at[m], index, rows), w[3, cols, :]), mlp.at[m])

    gg = Gather(p, gm0, agg_s, agg_r, rows)

    def stage_end(m):
        sc_m[m].finish()

        def body(i, carry):
            at = pl.ds(pl.multiple_of(i * chunk, chunk), chunk)
            a = mlp[m, at, :] + rbuf[m, 1, at, :].astype(F32) + rbuf[m, 2, at, :].astype(F32)
            h = midf[m, at, :]
            ra = lax.rsqrt(mean_sq(a) + 1e-06)
            na = a * ra
            al = vec[2:3, :]
            zz = h + al * (na - h)
            rz = lax.rsqrt(mean_sq(zz) + 1e-06)
            out = zz * rz
            outv[m, at, :] = out.astype(BF16)
            cot = ogv[m, at, :].astype(F32)
            dz = rz * (cot - out * jnp.mean(cot * out, axis=-1, keepdims=True))
            dn = al * dz
            acc[0:8, :] += fold8(dz * (na - h))
            gmd[m, at, :] = dz - dn
            grad = (ra * (dn - na * jnp.mean(dn * na, axis=-1, keepdims=True))).astype(BF16)
            gm[m, at, :] = grad
            if m == 0:
                gm0[pl.ds(pl.multiple_of(p.t * rows + i * chunk, chunk), chunk), :] = grad
            return carry

        lax.fori_loop(0, rows // chunk, body, 0)
        if m == 0:
            gg.start(gg.at(p.t))

    stage_qkv(0)
    attend(0)
    relay(1)
    stage_o(0)
    stage_qkv(1)
    attend(1)
    stage_mid(0)
    stage_o(1)
    relay(2)
    for m in range(mbs):
        ocopy(x.at[m], o_x.at[m])
        ocopy(q.at[m], o_q.at[m])
        ocopy(k.at[m], o_k.at[m])
        ocopy(v.at[m], o_v.at[m])
        ocopy(rq.at[m], o_rq.at[m])
        ocopy(rk.at[m], o_rk.at[m])
        ocopy(mixed.at[m], o_mixed.at[m])
    ocopy(vec, o_vec)
    ocopy(tab, o_tab)
    ocopy(ir, o_ir)
    relay(3)
    wready(1)
    wready(2)
    stage_up(0)
    stage_mid(1)
    wready(3)
    stage_down(0)
    stage_up(1)
    stage_down(1)
    og_in.wait()
    stage_end(0)
    ocopy(mid.at[0], o_mid.at[0])
    ocopy(up.at[0], o_up.at[0])
    ocopy(gate.at[0], o_gate.at[0])
    ocopy(inner.at[0], o_inner.at[0])
    for m in range(mbs):
        lrow = jnp.transpose(lcol[m], (1, 0))
        lcol[m, 0:8, 0:128] = lrow[0:8, 0:128]
        for j in range(1, seq // 128):
            lcol[m, 8 * j : 8 * j + 8, 0:128] = lrow[0:8, 128 * j : 128 * j + 128]
        ocopy(lcol.at[m, pl.ds(0, seq // 16)], o_lrow.at[m])
    ocopy(mid.at[1], o_mid.at[1])
    ocopy(up.at[1], o_up.at[1])
    ocopy(gate.at[1], o_gate.at[1])
    ocopy(inner.at[1], o_inner.at[1])
    ocopy(attn, o_attn)
    for step in range(1, 3):
        gg.wait(step)
    stage_end(1)
    ocopy(outv, o_out)
    ocopy(gmd, o_gmd)
    ocopy(gm, o_gm)
    ocopy(acc, o_acc)
    gg.wait(3)
    ocopy(gm0, o_gm0)
    for gather in gx + gmi + [gg]:
        gather.drain()
    for copy in sends + small_t + small_d:
        copy.wait_send()
    for copy in outs:
        copy.wait()


def bwd_kernel(
    n,
    hid, i_w, i_x, i_q, i_k, i_v, i_rq, i_rk, i_lrow, i_mixed, i_mid, i_up, i_gate,
    i_inner, i_attn, i_gmd, i_gm, i_gm0, i_vec, i_acc, i_tab, i_ir,
    o_in, o_gq, o_gk, o_gv, o_go, o_gu, o_gg, o_gd, o_tv,
    w, q, k, v, rq, rk, lrow, mixed, up, gate, inner, attn, gmd, gm, ga, vec, acc,
    tab, ir, kt, dqt, dk, dv, outv, xrecv, zrecv, vsend, vrecv, tv, sbuf, rbuf,
    lsem, agg_s, agg_r, aga_s, aga_r, rsm_s, rsm_r, rsi_s, rsi_r, xs, xr, zs, zr, vs, vr, osem,
):
    p = Place(n)
    nz = p.nz
    mbs, rows, width = hid.shape
    seq = q.shape[1]
    hw = q.shape[2]
    heads = hw // DH
    hidden = up.shape[2]
    groups = w.shape[0]
    shard = width // n
    gmix = [inner.at[m, :, pl.ds(0, hw)] for m in range(mbs)]
    pts, dss = (inner.at[m, pl.ds(0, seq - 128), pl.ds(hw, heads * QB)] for m in range(2))
    qs, gs = (
        inner.at[0, pl.ds(i * heads * QB, heads * QB), pl.ds(hw + heads * QB, hw)] for i in range(2)
    )

    local = []

    def lcopy(src, dst):
        copy = pltpu.make_async_copy(src, dst, lsem.at[len(local)])
        copy.start()
        local.append(copy)
        return copy

    outs = []

    def ocopy(src, dst):
        copy = pltpu.make_async_copy(src, dst, osem.at[len(outs)])
        copy.start()
        outs.append(copy)

    l_gm0 = lcopy(i_gm0, gm.at[0])
    l_w3 = lcopy(i_w.at[3], w.at[3])
    l_ug = [[lcopy(i_up.at[m], up.at[m]), lcopy(i_gate.at[m], gate.at[m])] for m in range(mbs)]
    l_vec = [lcopy(i_vec, vec), lcopy(i_acc, acc)]
    p.barrier()
    gg = Gather(p, gm.at[1], agg_s, agg_r, rows)
    gg.start(i_gm.at[1])
    l_gm1 = lcopy(i_gm.at[1], gg.at(p.t))
    l_w12 = [lcopy(i_w.at[1], w.at[1]), lcopy(i_w.at[2], w.at[2])]
    l_inner = [lcopy(i_inner.at[m], inner.at[m]) for m in range(mbs)]
    l_rows = [lcopy(i_attn, attn), lcopy(i_gmd, gmd)]
    l_w0 = lcopy(i_w.at[0], w.at[0])
    l_att = [
        [
            lcopy(src.at[m], dst.at[m])
            for src, dst in ((i_q, q), (i_k, k), (i_v, v), (i_rq, rq), (i_rk, rk), (i_lrow, lrow), (i_mixed, mixed))
        ]
        for m in range(mbs)
    ]
    l_tab = [lcopy(i_tab, tab), lcopy(i_ir, ir)]

    gga = [Gather(p, ga.at[m], aga_s.at[m], aga_r.at[m], rows) for m in range(mbs)]
    l_hid = [lcopy(hid.at[m], gga[m].at(p.t)) for m in range(mbs)]
    sc_m = [Scatter(p, sbuf.at[m], rbuf.at[m], rsm_s.at[m], rsm_r.at[m]) for m in range(mbs)]
    sc_i = [Scatter(p, sbuf.at[m], rbuf.at[m], rsi_s.at[m], rsi_r.at[m]) for m in range(mbs)]
    cols = 256
    chunk = 32

    def stage_inner(m):
        if m == 1:
            l_gm1.wait()

        def work(index):
            at = pl.ds(pl.multiple_of(index * rows, rows), rows)

            def body(c, carry):
                lanes = pl.ds(pl.multiple_of(c * cols, cols), cols)
                gi = nn(gm[m, at, :], w[3, :, lanes])
                u = up[m, at, lanes].astype(F32)
                g = gate[m, at, lanes].astype(F32)
                su = vec[3:4, lanes]
                sg = vec[4:5, lanes]
                gsc = g * sg
                sig = 1.0 / (1.0 + jnp.exp(-gsc))
                gu = gi * (gsc * sig)
                ggs = gi * (u * su) * sig * (1.0 + gsc * (1.0 - sig))
                acc[16:24, lanes] += fold8(gu * u)
                acc[24:32, lanes] += fold8(ggs * g)
                up[m, at, lanes] = (gu * su).astype(BF16)
                gate[m, at, lanes] = (ggs * sg).astype(BF16)
                return carry

            lax.fori_loop(0, hidden // cols, body, 0)

        blocks(p, work, gg.wait if m == 1 else None)

    def stage_back(m):
        sc_m[m].run(
            lambda index, cols: nt(rows_of(up.at[m], index, rows), w[1, cols, :])
            + nt(rows_of(gate.at[m], index, rows), w[2, cols, :]),
            outv.at[m],
        )

    def stage_attn(m):
        sc_m[m].finish()
        base = p.t * rows

        def body(i, carry):
            at = pl.ds(pl.multiple_of(i * chunk, chunk), chunk)
            own = pl.ds(pl.multiple_of(base + i * chunk, chunk), chunk)
            part = outv[m, at, :] + rbuf[m, 1, at, :].astype(F32)
            cot = gmd[m, at, :] + part + rbuf[m, 2, at, :].astype(F32)
            a = attn[m, at, :]
            h = ga[m, own, :].astype(F32)
            ra = lax.rsqrt(mean_sq(a) + 1e-06)
            na = a * ra
            al = vec[1:2, :]
            zz = h + al * (na - h)
            rz = lax.rsqrt(mean_sq(zz) + 1e-06)
            out = zz * rz
            dz = rz * (cot - out * jnp.mean(cot * out, axis=-1, keepdims=True))
            dn = al * dz
            acc[8:16, :] += fold8(dz * (na - h))
            gmd[m, at, :] = dz - dn
            ga[m, own, :] = (ra * (dn - na * jnp.mean(dn * na, axis=-1, keepdims=True))).astype(BF16)
            return carry

        lax.fori_loop(0, rows // chunk, body, 0)
        gga[m].start(gga[m].at(p.t))

    def stage_mixed(m):
        def work(index):
            at = pl.ds(pl.multiple_of(index * rows, rows), rows)
            gmix[m][at, :] = nn(ga[m, at, :], w[0, :, 3 * hw : 4 * hw]).astype(BF16)

        gga[m].each(work)

    win = seq - 128
    c_exp = math.sqrt(DH) * LOG2E
    ones = head_ones()

    def attend(m):
        kt[...] = jnp.transpose(k[m], (1, 0))
        dk[...] = jnp.zeros_like(dk)
        dv[...] = jnp.zeros_like(dv)

        def body(b, carry):
            at = pl.ds(pl.multiple_of(b * QB, QB), QB)
            keys = pl.ds(pl.multiple_of(((b + 3) // 8) * 128, 128), win)
            crow = ir[m, 0:1, at]
            lrow_ = ir[m, 1:2, at]
            ccol = tab[m, keys, DH : DH + 1]
            bias = jnp.where((ccol <= crow) & (ccol >= lrow_), 0.0, -1e30)
            qb = q[m, at, :]
            gb = gmix[m][at, :]
            lane = lane_iota((QB, hw)) // DH
            for h in range(heads):
                qs[h * QB : (h + 1) * QB, :] = jnp.where(lane == h, qb, jnp.zeros_like(qb))
                gs[h * QB : (h + 1) * QB, :] = jnp.where(lane == h, gb, jnp.zeros_like(gb))
            kb = k[m, keys, :]
            vb = v[m, keys, :]
            for h in range(heads):
                hl = slice(h * QB, (h + 1) * QB)
                scores = nt(kb, qs[hl, :])
                inv = lrow[m, pl.ds(pl.multiple_of(b * 8, 8), 8), :][h : h + 1, :]
                pt = jnp.exp2(scores * c_exp + bias) * inv
                dpt = nt(vb, gs[hl, :])
                delta = jnp.sum(pt * dpt, axis=0, keepdims=True)
                dst = (pt * (dpt - delta)).astype(BF16)
                pts[:, hl] = pt.astype(BF16)
                dss[:, hl] = dst
                dqt[h * DH : (h + 1) * DH, at] = nn(kt[h * DH : (h + 1) * DH, keys], dst)
            dv[keys, :] += nn(pts[...], gs[...])
            dk[keys, :] += nn(dss[...], qs[...])
            return carry

        lax.fori_loop(0, seq // QB, body, 0)

        step = 256

        def after(i, carry):
            at = pl.ds(pl.multiple_of(i * step, step), step)
            cb, sb = turns(tab[m, at, :])
            v[m, at, :] = dv[at, :].astype(BF16)
            for which in range(2):
                src = (q, k)[which]
                rsc = (rq, rk)[which]
                for half in range(hw // 128):
                    lanes = slice(128 * half, 128 * half + 128)
                    if which == 0:
                        grad = jnp.transpose(dqt[lanes, at], (1, 0)) * math.sqrt(DH)
                    else:
                        grad = dk[at, lanes] * math.sqrt(DH)
                    gain = vec[0:1, lanes]
                    unit = src[m, at, lanes].astype(F32) / gain
                    acc[32:40, lanes] += fold8(grad * unit)
                    dn = grad * gain
                    dy = rsc[m, at, lanes].astype(F32) * (dn - unit * split_sum(dn * unit, ones))
                    src[m, at, lanes] = (dy * cb - partner(dy) * sb).astype(BF16)
            return carry

        lax.fori_loop(0, seq // step, after, 0)

    def stage_in(m):
        def part(index, cols):
            at = pl.ds(pl.multiple_of(index * rows, rows), rows)
            return (
                nt(q[m, at, :], w[0, cols, 0:hw])
                + nt(k[m, at, :], w[0, cols, hw : 2 * hw])
                + nt(v[m, at, :], w[0, cols, 2 * hw : 3 * hw])
            )

        sc_i[m].run(part, outv.at[m])

    def stage_out(m):
        sc_i[m].finish()

        def body(i, carry):
            at = pl.ds(pl.multiple_of(i * chunk, chunk), chunk)
            part = outv[m, at, :] + rbuf[m, 1, at, :].astype(F32)
            total = gmd[m, at, :] + part + rbuf[m, 2, at, :].astype(F32)
            sbuf[m, 0, at, :] = total.astype(BF16)
            return carry

        lax.fori_loop(0, rows // chunk, body, 0)
        ocopy(sbuf.at[m, 0], o_in.at[m])

    pieces = {
        3: (w.at[3], 3, 0, width),
        1: (w.at[1], 1, 0, width),
        2: (w.at[2], 2, 0, width),
        0: (gm.at[0], 0, 0, 3 * hw),
        4: (gm.at[0], 0, 3 * hw, 4 * hw),
    }

    def weight_grad(key, left, rights):
        into = pieces[key][0]

        def body(c, carry):
            lanes = pl.ds(pl.multiple_of(c * cols, cols), cols)
            for lo, hi, right in rights:
                total = tn(left[0, :, lanes], right[0])
                for m in range(1, mbs):
                    total = total + tn(left[m, :, lanes], right[m])
                into[lanes, lo:hi] = total.astype(BF16)
            return carry

        lax.fori_loop(0, width // cols, body, 0)

    def wrow(key, index):
        ref, _, lo, hi = pieces[key]
        return ref.at[pl.ds(pl.multiple_of(index * shard, shard), shard), pl.ds(lo, hi - lo)]

    def held(buf, key, index):
        _, g, lo, hi = pieces[key]
        return buf.at[g, index, :, pl.ds(lo, hi - lo)]

    gsends = []

    def rs_start(key):
        for kk in list(range(1, nz)) + [0]:
            zz = (p.z + kk) % nz
            other = 2 * zz + 1 - p.xi
            copy = remote(wrow(key, other), held(xrecv, key, zz), xs.at[key, kk], xr.at[key, zz], dp=p.xn)
            copy.start()
            gsends.append(copy)

    def rs_arrive(key, kk):
        zz = (p.z + kk) % nz
        got = held(xrecv, key, zz)
        remote(got, got, xs.at[key, kk], xr.at[key, zz], dp=p.xn).wait_recv()
        return got, zz

    def rs_mid(key):
        for kk in range(1, nz):
            got, zz = rs_arrive(key, kk)
            mine = 2 * zz + p.xi
            got[...] = (got[...].astype(F32) + wrow(key, mine)[...].astype(F32)).astype(BF16)
            copy = remote(got, held(zrecv, key, kk - 1), zs.at[key, kk - 1], zr.at[key, kk - 1], dp=mine)
            copy.start()
            gsends.append(copy)

    def rs_end(key):
        _, g, lo, hi = pieces[key]
        got, _ = rs_arrive(key, 0)
        total = got[...].astype(F32) + wrow(key, p.d)[...].astype(F32)
        for kk in range(1, nz):
            got = held(zrecv, key, kk - 1)
            remote(got, got, zs.at[key, kk - 1], zr.at[key, kk - 1], dp=p.xn).wait_recv()
            total = total + got[...].astype(F32)
        fin = attn.at[g // 2, pl.ds((g % 2) * shard, shard)]
        fin[:, lo:hi] = total
        if g == 0:
            for i, dst in enumerate((o_gq, o_gk, o_gv, o_go)):
                if lo <= i * hw < hi:
                    ocopy(fin.at[:, pl.ds(i * hw, hw)], dst)
        else:
            ocopy(fin, (o_gu, o_gg, o_gd)[g - 1])

    for copy in l_vec + [l_gm0, l_w3] + l_ug[0]:
        copy.wait()
    stage_inner(0)
    for copy in l_w12:
        copy.wait()
    stage_back(0)
    for copy in l_ug[1]:
        copy.wait()
    stage_inner(1)
    for copy in l_inner + l_rows + l_hid:
        copy.wait()
    weight_grad(3, gm, [(0, hidden, inner)])
    rs_start(3)
    gg.drain()
    l_mid = [lcopy(i_mid.at[m], gm.at[m]) for m in range(mbs)]
    stage_attn(0)
    stage_back(1)
    for copy in l_mid:
        copy.wait()
    weight_grad(1, gm, [(0, hidden, up)])
    rs_start(1)
    l_x = [lcopy(i_x.at[m], up.at[m]) for m in range(mbs)]
    for copy in [l_w0] + l_tab + l_att[0] + l_att[1]:
        copy.wait()
    stage_mixed(0)
    rs_mid(3)
    attend(0)
    stage_attn(1)
    stage_in(0)
    weight_grad(2, gm, [(0, hidden, gate)])
    rs_start(2)
    rs_mid(1)
    stage_mixed(1)
    weight_grad(4, ga, [(3 * hw, 4 * hw, mixed)])
    rs_start(4)
    attend(1)
    rs_mid(2)

    per = width // 128
    for r in range(5):
        sums = jnp.sum(acc[8 * r : 8 * r + 8, :], axis=0, keepdims=True)
        for j in range(per):
            vsend[per * r + j : per * r + j + 1, :] = sums[:, 128 * j : 128 * j + 128]
    vcopies = []
    for i, peer in enumerate(p.dpeers):
        copy = remote(vsend, vrecv.at[i], vs.at[i], vr.at[i], dp=peer)
        copy.start()
        vcopies.append(copy)
    for copy in l_x:
        copy.wait()
    weight_grad(0, up, [(0, hw, q), (hw, 2 * hw, k), (2 * hw, 3 * hw, v)])
    rs_start(0)
    rs_mid(4)
    stage_in(1)
    stage_out(0)
    rs_mid(0)
    total = vsend[...]
    for i in range(n - 1):
        remote(vrecv.at[i], vrecv.at[i], vs.at[i], vr.at[i], dp=p.xn).wait_recv()
        total = total + vrecv[i]
    tv[p.t] = total
    for i, peer in enumerate(p.tpeers):
        copy = remote(tv.at[p.t], tv.at[p.t], vs.at[n - 1 + i], vr.at[n - 1 + i], tensor=peer)
        copy.start()
        vcopies.append(copy)
    rs_end(3)
    rs_end(1)
    rs_end(2)
    stage_out(1)
    for i, peer in enumerate(p.tpeers):
        src = (p.t + 4 - (i + 1)) % 4
        remote(tv.at[src], tv.at[src], vs.at[n - 1 + i], vr.at[n - 1 + i], tensor=peer).wait_recv()
    ocopy(tv, o_tv)
    rs_end(4)
    rs_end(0)
    for gather in gga:
        gather.drain()
    for copy in gsends + vcopies:
        copy.wait_send()
    for copy in outs:
        copy.wait()


def out_kernel(turned, hw, i_tv, *refs):
    count = (len(refs) - 8 - turned) // 3
    ins, outs, vecs = refs[:count], refs[count : 2 * count], refs[2 * count : 2 * count + 5]
    tv, isem, osem = refs[2 * count + 5], refs[-2], refs[-1]
    bufs = refs[2 * count + 6 : -2]
    tv_in = pltpu.make_async_copy(i_tv, tv, isem.at[count])
    tv_in.start()
    loads = [pltpu.make_async_copy(ins[i], bufs[i], isem.at[i]) for i in range(count)]
    for copy in loads:
        copy.start()
    stores = []
    for i, copy in enumerate(loads):
        copy.wait()
        buf = bufs[i]
        if i >= count - turned:
            buf = bufs[turned + i]
            buf[...] = jnp.transpose(bufs[i][...], (1, 0))
        stores.append(pltpu.make_async_copy(buf, outs[i], osem.at[i]))
        stores[-1].start()
    tv_in.wait()
    flat = 4 * lax.axis_index("dp") + lax.axis_index("tensor")
    per = tv.shape[1] // 5
    for ref, row, whole in zip(vecs, (4, 1, 0, 2, 3), (hw, 0, 0, per * 128, per * 128)):
        size = ref.shape[1]
        start = flat * size
        if whole:
            line = per * row + start % whole // 128
            part = tv[start // whole, pl.ds(line, 1), :]
        else:
            line = per * row + start // 128
            part = tv[0, pl.ds(line, 1), :]
            for a in range(1, tv.shape[0]):
                part = part + tv[a, pl.ds(line, 1), :]
        part = pltpu.roll(jnp.broadcast_to(part, (8, 128)), (128 - start % 128) % 128, 1)
        ref[...] = part[0:1, :size]
    for copy in stores:
        copy.wait()


def shards(
    hidden_in, out_grad, doc_ids, w_query, w_key, w_value, w_output, w_up, w_gate, w_down,
    scale_qk, alpha_attn, alpha_mlp, scale_up, scale_gate,
):
    n = lax.axis_size("dp")
    mbs, rows, width = hidden_in.shape
    seq = doc_ids.shape[2]
    hw = w_query.shape[1]
    hidden = w_up.shape[1]
    shard = w_query.shape[0]
    nz = n // 2
    flat = 4 * lax.axis_index("dp") + lax.axis_index("tensor")

    small = jnp.stack(
        [jnp.pad(item, (0, 128 - item.shape[0])) for item in (scale_qk, alpha_attn, alpha_mlp, scale_up, scale_gate)]
        + [jnp.zeros((128,), F32)] * 3
    )

    any_ = pl.BlockSpec(memory_space=pl.ANY)
    vm = pltpu.VMEM
    dma = pltpu.SemaphoreType.DMA

    def sds(shape, dtype):
        return jax.ShapeDtypeStruct(shape, dtype)

    res_shapes = dict(
        out=((mbs, rows, width), BF16),
        w=((4, width, width), BF16),
        x=((mbs, seq, width), BF16),
        q=((mbs, seq, hw), BF16),
        k=((mbs, seq, hw), BF16),
        v=((mbs, seq, hw), BF16),
        rq=((mbs, seq, hw), BF16),
        rk=((mbs, seq, hw), BF16),
        lrow=((mbs, seq // 16, 128), F32),
        mixed=((mbs, seq, hw), BF16),
        mid=((mbs, seq, width), BF16),
        up=((mbs, seq, hidden), BF16),
        gate=((mbs, seq, hidden), BF16),
        inner=((mbs, seq, hidden), BF16),
        attn=((mbs, rows, width), F32),
        gmd=((mbs, rows, width), F32),
        gm=((mbs, rows, width), BF16),
        gm0=((seq, width), BF16),
        vec=((8, width), F32),
        acc=((40, width), F32),
        tab=((mbs, seq, 128), F32),
        ir=((mbs, 8, seq), F32),
    )
    r = {key: sds(*val) for key, val in res_shapes.items()}
    s = {key: vm(*val) for key, val in res_shapes.items()}
    nvec = 5 * (width // 128)
    own32 = vm((mbs, rows, width), F32)
    scat = [vm((mbs, 3, rows, width), BF16), vm((mbs, 3, rows, width), BF16)]
    heads = hw // DH
    res = pl.pallas_call(
        functools.partial(fwd_kernel, n),
        name="fwd",
        out_shape=tuple(r.values()),
        in_specs=[any_] * 11,
        out_specs=tuple([any_] * len(r)),
        scratch_shapes=[
            s["w"], s["x"], s["q"], s["k"], s["v"], s["rq"], s["rk"],
            vm((mbs, seq, 128), F32),
            s["mixed"], s["mid"], s["up"], s["gate"], s["inner"],
            s["attn"], own32, own32, s["gmd"], s["gm"], s["gm0"], s["vec"], s["acc"],
            s["tab"], s["ir"],
            vm((4 * n, 8, 128), F32),
            vm((mbs, 1, seq), jnp.int32),
            vm((mbs, rows, width), BF16), vm((mbs, rows, width), BF16),
            vm((heads * QB, hw), BF16),
            *scat,
            dma((4, n)), dma((4, n)),
            dma((n + 2,)), dma((n + 2,)),
            dma((16,)),
            dma((mbs, 3)), dma((mbs, 3)), dma((mbs, 3)), dma((mbs, 3)), dma((3,)), dma((3,)),
            dma((mbs, 3)), dma((mbs, 3)), dma((mbs, 3)), dma((mbs, 3)),
            dma((40,)),
        ],
        compiler_params=pltpu.CompilerParams(
            collective_id=0, has_side_effects=True, vmem_limit_bytes=VMEM_LIMIT
        ),
    )(w_query, w_key, w_value, w_output.T, w_up, w_gate, w_down.T, hidden_in, out_grad, small, doc_ids)
    r = dict(zip(r, res))

    gshape = sds((shard, hw), F32)
    fshape = sds((shard, hidden), F32)
    grads = pl.pallas_call(
        functools.partial(bwd_kernel, n),
        name="bwd",
        out_shape=(
            sds((mbs, rows, width), BF16), gshape, gshape, gshape, gshape, fshape, fshape, fshape,
            sds((4, nvec, 128), F32),
        ),
        in_specs=[any_] * 22,
        out_specs=tuple([any_] * 9),
        scratch_shapes=[
            s["w"], s["q"], s["k"], s["v"], s["rq"], s["rk"], s["lrow"], s["mixed"],
            s["up"], s["gate"], s["inner"], s["attn"], s["gmd"],
            s["x"], s["x"], s["vec"], s["acc"],
            s["tab"], s["ir"],
            vm((hw, seq), BF16), vm((hw, seq), F32), vm((seq, hw), F32), vm((seq, hw), F32),
            own32,
            vm((4, nz, shard, width), BF16), vm((4, nz - 1, shard, width), BF16),
            vm((nvec, 128), F32), vm((n - 1, nvec, 128), F32), vm((4, nvec, 128), F32),
            *scat,
            dma((48,)), dma((3,)), dma((3,)), dma((mbs, 3)), dma((mbs, 3)),
            dma((mbs, 3)), dma((mbs, 3)), dma((mbs, 3)), dma((mbs, 3)),
            dma((5, nz)), dma((5, nz)), dma((5, nz - 1)), dma((5, nz - 1)),
            dma((n + 2,)), dma((n + 2,)),
            dma((16,)),
        ],
        compiler_params=pltpu.CompilerParams(
            collective_id=1, has_side_effects=True, vmem_limit_bytes=VMEM_LIMIT
        ),
    )(
        hidden_in, r["w"], r["x"], r["q"], r["k"], r["v"], r["rq"], r["rk"], r["lrow"],
        r["mixed"], r["mid"], r["up"], r["gate"], r["inner"], r["attn"], r["gmd"], r["gm"], r["gm0"],
        r["vec"], r["acc"], r["tab"], r["ir"],
    )
    g_in, gq, gk, gv, go, gu, gg, gd, tv = grads
    results = [gq, gk, gv, gu, gg, r["out"], g_in, go, gd]
    turned = 2 if shard % 128 == 0 else 0
    if not turned:
        results = results[:-2]
    finals = [sds(item.shape, item.dtype) for item in results]
    for i in range(len(results) - turned, len(results)):
        finals[i] = sds(finals[i].shape[::-1], F32)
    ones = [scale_qk, alpha_attn, alpha_mlp, scale_up, scale_gate]
    done = pl.pallas_call(
        functools.partial(out_kernel, turned, hw),
        name="results",
        out_shape=tuple(finals) + tuple(sds((1, item.shape[0]), F32) for item in ones),
        in_specs=[any_] * (len(results) + 1),
        out_specs=(any_,) * len(finals) + (pl.BlockSpec(memory_space=vm),) * 5,
        scratch_shapes=[
            vm(tv.shape, F32),
            *[vm(item.shape, item.dtype) for item in results],
            *[vm(item.shape, item.dtype) for item in finals[len(results) - turned :]],
            dma((len(results) + 1,)), dma((len(results),)),
        ],
        compiler_params=pltpu.CompilerParams(vmem_limit_bytes=VMEM_LIMIT // 2),
    )(tv, *results)
    vecs = [item.reshape(-1) for item in done[len(finals) :]]
    gq, gk, gv, gu, gg, out, g_in = done[:7]
    go, gd = done[7:9] if turned else (go.T, gd.T)
    return (out, g_in, gq, gk, gv, go, gu, gg, gd, *vecs)


def solution(mesh):
    rows = P("dp", "tensor", None)
    inward = P("dp", "tensor")
    outward = P("tensor", "dp")
    flat = P(("dp", "tensor"))
    weights = (inward, inward, inward, outward, inward, inward, outward)
    in_specs = (rows, rows, P("dp", None, None)) + weights + (flat,) * 5
    out_specs = (rows, rows) + weights + (flat,) * 5
    return jax.shard_map(shards, mesh=mesh, in_specs=in_specs, out_specs=out_specs, check_vma=False)
```

profile of v0, /device:TPU:0, one launch (start us, length us, event | category | flops | bytes accessed | tf_op | source)
XLA Modules:
  0.0 377.6 jit_solution(18428983011637963717)
XLA Ops:
  0.6 0.7 pad_bitcast_fusion.2
  1.3 0.7 pad_bitcast_fusion
  2.0 1.3 stack.27.small
  3.3 1.6 copy.29
  4.8 1.8 copy.30
  6.6 182.1 %fwd.1 = (bf16[2,256,1024]{2,1,0:T(8,128)(2,1)}, bf16[4,1024,1024]{2,1,0:T(8,128)(2,1)}, bf16[2,1024,1024]{2,1,0:T(8,128)(2,1)}, bf16[2,1024,256]{2,1,0:T(8,128)...) custom-call(bf16[128,256]{1,0:T(8,128)(2,1)} %wq.1, ...), custom_call_target="tpu_custom_call" | custom-call | tf_op jit(solution)/shard_map/fwd/pallas_call | solution.py:1052
  188.8 174.7 %bwd.1 = (bf16[2,256,1024]{2,1,0:T(8,128)(2,1)}, f32[128,256]{1,0:T(8,128)}, f32[128,256]{1,0:T(8,128)}, f32[128,256]{1,0:T(8,128)}, f32[128,256]{1,0:T(8,128)},...) custom-call(bf16[2,256,1024]{2,1,0:T(8,128)(2,1)} %hid.3, ...), custom_call_target="tpu_custom_call" | custom-call | tf_op jit(solution)/shard_map/bwd/pallas_call | solution.py:1084
  363.5 0.0 copy-start
  363.5 1.2 copy-done
  364.7 0.0 copy-start.1
  364.7 1.2 copy-done.1
  365.9 0.0 copy-start.2
  365.9 1.0 copy-done.2
  367.0 0.0 copy-start.3
  367.0 1.0 copy-done.3
  368.0 0.0 copy-start.4
  368.0 1.0 copy-done.4
  369.1 0.0 copy-start.5
  369.1 0.9 copy-done.5
  370.0 0.0 copy-start.6
  370.0 0.9 copy-done.6
  370.9 0.0 copy-start.7
  370.9 0.9 copy-done.7
  371.8 0.0 copy-start.8
  371.8 0.9 copy-done.8
  372.7 0.0 copy-start.9
  372.7 0.9 copy-done.9
  373.6 3.8 %results.1 = (f32[128,256]{1,0:T(8,128)}, f32[128,256]{1,0:T(8,128)}, f32[128,256]{1,0:T(8,128)}, f32[128,1024]{1,0:T(8,128)}, f32[128,1024]{1,0:T(8,128)}, /*in...) custom-call(f32[4,40,128]{2,1,0:T(8,128)S(1)} %copy-done.9, ...), custom_call_target="tpu_custom_call" | custom-call | tf_op jit(solution)/shard_map/results/pallas_call | solution.py:1126
  (2 shorter events, 0.0 us)
Async XLA Ops:
  363.5 1.2 copy-start
  364.7 1.2 copy-start.1
  365.9 1.0 copy-start.2
  367.0 1.0 copy-start.3
  368.0 1.0 copy-start.4
  369.1 0.9 copy-start.5
  370.0 0.9 copy-start.6
  370.9 0.9 copy-start.7
  371.8 0.9 copy-start.8
  372.7 0.9 copy-start.9
where the time goes:
time: 380 us; the launch traced here: 378 us
  Pallas kernels  361 us (95%)
  local copies, waits for them, and re-layouts  16 us (4%)
    pallas_call x1, Pallas kernels, shards(): pl.pallas_call(functools.partial(fwd_kernel, n), name='fwd', out_shape=tu...  182 us
    pallas_call x1, Pallas kernels, shards(): pl.pallas_call(functools.partial(bwd_kernel, n), name='bwd', out_shape=(s...  175 us
    unnamed x22, local copies, waits for them, and re-layouts  13.4 us

commit v1 on v0

--- a/solution.py
+++ b/solution.py
@@ -18,7 +18,7 @@
 VMEM_LIMIT = 67043328
 LOG2E = 1.4426950408889634
 QB = 128
-COLS = 256
+WIDE = 512
 CODE = 8
 
 
@@ -147,59 +147,38 @@
 class Scatter:
     def __init__(self, place, sbuf, rbuf, ssem, rsem):
         self.p, self.sbuf, self.rbuf, self.ssem, self.rsem = place, sbuf, rbuf, ssem, rsem
-        self.copies = []
-
-    def send(self, slot, **where):
-        copy = remote(
-            self.sbuf.at[slot], self.rbuf.at[slot], self.ssem.at[slot], self.rsem.at[slot], **where
-        )
-        copy.start()
-        self.copies.append(copy)
+
+    def copy(self, slot):
+        where = self.p.yp if slot == 2 else self.p.sib
+        return remote(self.sbuf.at[slot], self.rbuf.at[slot], self.ssem.at[slot], self.rsem.at[slot], tensor=where)
 
     def arrive(self, slot):
-        remote(
-            self.rbuf.at[slot], self.rbuf.at[slot], self.ssem.at[slot], self.rsem.at[slot],
-            tensor=self.p.sib,
-        ).wait_recv()
+        self.copy(slot).wait_recv()
 
     def run(self, part, own):
         p = self.p
-        width = own.shape[1]
-
-        def fill(index, put):
-            def body(c, carry):
-                lanes = pl.ds(pl.multiple_of(c * COLS, COLS), COLS)
-                put(lanes, part(index, lanes))
-                return carry
-
-            lax.fori_loop(0, width // COLS, body, 0)
-
-        def first(slot):
-            def put(lanes, vals):
-                self.sbuf[slot, :, lanes] = vals.astype(BF16)
-
-            return put
-
-        def across(lanes, vals):
-            self.sbuf[2, :, lanes] = (vals + self.rbuf[0, :, lanes].astype(F32)).astype(BF16)
-
-        def mine(lanes, vals):
-            own[:, lanes] = vals
-
-        fill(p.diag, first(0))
-        self.send(0, tensor=p.sib)
-        fill(p.sib, first(1))
-        self.send(1, tensor=p.sib)
-        self.arrive(0)
-        fill(p.yp, across)
-        self.send(2, tensor=p.yp)
-        fill(p.t, mine)
+
+        def send(slot):
+            vals = own[...]
+            if slot == 2:
+                self.arrive(0)
+                vals = vals + self.rbuf[0].astype(F32)
+            self.sbuf[slot] = vals.astype(BF16)
+            self.copy(slot).start()
+
+        def body(i, carry):
+            own[...] = part((p.t // 2 + (i + 1) % 2) % 2 * 2 + (p.t + 1 - i // 2) % 2)
+            for slot in range(3):
+                pl.when(i == slot)(functools.partial(send, slot))
+            return carry
+
+        lax.fori_loop(0, 4, body, 0)
 
     def finish(self):
         self.arrive(1)
         self.arrive(2)
-        for copy in self.copies:
-            copy.wait_send()
+        for slot in range(3):
+            self.copy(slot).wait_send()
 
 
 def rows_of(ref, index, rows):
@@ -237,8 +216,11 @@
     groups = w.shape[0]
     hidden = up.shape[2]
 
-    def wat(g, index):
-        return w.at[g, pl.ds(pl.multiple_of(index * shard, shard), shard)]
+    pieces = ((0, 0, 3 * hw), (0, 3 * hw, 4 * hw), (1, 0, hidden), (2, 0, hidden), (3, 0, hidden))
+
+    def wat(key, index):
+        g, lo, hi = pieces[key]
+        return w.at[g, pl.ds(pl.multiple_of(index * shard, shard), shard), pl.ds(lo, hi - lo)]
 
     local = []
 
@@ -286,7 +268,7 @@
 
     for copy in w_in:
         copy.wait()
-    for g in range(groups):
+    for g in range(len(pieces)):
         for i, peer in enumerate(p.zpeers):
             wsend_to(g, i, wat(g, p.d), p.d, peer)
         if g == 0:
@@ -310,7 +292,9 @@
         for peer in p.zpeers:
             other = peer + 1 - 2 * p.xi
             remote(wat(g, other), wat(g, other), wsend.at[g, 0], wrecv.at[g, other], dp=p.xn).wait_recv()
-        ocopy(w.at[g], o_w.at[g])
+        if g:
+            g, _, _ = pieces[g]
+            ocopy(w.at[g], o_w.at[g])
 
     docs_in.wait()
     for m in range(mbs):
@@ -342,7 +326,7 @@
     acc[...] = jnp.zeros_like(acc)
 
     relay(0)
-    for g in range(1, groups):
+    for g in range(1, len(pieces)):
         wsend_to(g, nz - 1, wat(g, p.d), p.d, p.xn)
     for i, peer in enumerate(p.tpeers):
         part = sall.at[pl.ds((p.t + 4 - (i + 1)) % 4 * n, n)]
@@ -430,7 +414,7 @@
 
     def stage_o(m):
         sc_a[m].run(
-            lambda index, cols: nt(rows_of(mixed.at[m], index, rows), w[0, cols, 3 * hw : 3 * hw + hw]),
+            lambda index: nt(rows_of(mixed.at[m], index, rows), w[0, :, 3 * hw : 3 * hw + hw]),
             attn.at[m],
         )
 
@@ -456,14 +440,13 @@
         lax.fori_loop(0, rows // chunk, body, 0)
         gmi[m].start(gmi[m].at(p.t))
 
-    cols = 256
 
     def stage_up(m):
         def work(index):
             at = pl.ds(pl.multiple_of(index * rows, rows), rows)
 
             def body(c, carry):
-                lanes = pl.ds(pl.multiple_of(c * cols, cols), cols)
+                lanes = pl.ds(pl.multiple_of(c * WIDE, WIDE), WIDE)
                 mb = mid[m, at, :]
                 u = nn(mb, w[1, :, lanes])
                 g = nn(mb, w[2, :, lanes])
@@ -473,12 +456,12 @@
                 inner[m, at, lanes] = ((u * vec[3:4, lanes]) * (gs / (1.0 + jnp.exp(-gs)))).astype(BF16)
                 return carry
 
-            lax.fori_loop(0, hidden // cols, body, 0)
+            lax.fori_loop(0, hidden // WIDE, body, 0)
 
         gmi[m].each(work)
 
     def stage_down(m):
-        sc_m[m].run(lambda index, cols: nt(rows_of(inner.at[m], index, rows), w[3, cols, :]), mlp.at[m])
+        sc_m[m].run(lambda index: nt(rows_of(inner.at[m], index, rows), w[3]), mlp.at[m])
 
     gg = Gather(p, gm0, agg_s, agg_r, rows)
 
@@ -512,14 +495,16 @@
             gg.start(gg.at(p.t))
 
     stage_qkv(0)
+    relay(1)
     attend(0)
-    relay(1)
+    relay(2)
+    wready(1)
     stage_o(0)
     stage_qkv(1)
     attend(1)
     stage_mid(0)
+    relay(3)
     stage_o(1)
-    relay(2)
     for m in range(mbs):
         ocopy(x.at[m], o_x.at[m])
         ocopy(q.at[m], o_q.at[m])
@@ -531,12 +516,12 @@
     ocopy(vec, o_vec)
     ocopy(tab, o_tab)
     ocopy(ir, o_ir)
-    relay(3)
-    wready(1)
+    relay(4)
     wready(2)
+    wready(3)
     stage_up(0)
     stage_mid(1)
-    wready(3)
+    wready(4)
     stage_down(0)
     stage_up(1)
     stage_down(1)
@@ -649,7 +634,7 @@
             at = pl.ds(pl.multiple_of(index * rows, rows), rows)
 
             def body(c, carry):
-                lanes = pl.ds(pl.multiple_of(c * cols, cols), cols)
+                lanes = pl.ds(pl.multiple_of(c * WIDE, WIDE), WIDE)
                 gi = nn(gm[m, at, :], w[3, :, lanes])
                 u = up[m, at, lanes].astype(F32)
                 g = gate[m, at, lanes].astype(F32)
@@ -665,14 +650,14 @@
                 gate[m, at, lanes] = (ggs * sg).astype(BF16)
                 return carry
 
-            lax.fori_loop(0, hidden // cols, body, 0)
+            lax.fori_loop(0, hidden // WIDE, body, 0)
 
         blocks(p, work, gg.wait if m == 1 else None)
 
     def stage_back(m):
         sc_m[m].run(
-            lambda index, cols: nt(rows_of(up.at[m], index, rows), w[1, cols, :])
-            + nt(rows_of(gate.at[m], index, rows), w[2, cols, :]),
+            lambda index: nt(rows_of(up.at[m], index, rows), w[1])
+            + nt(rows_of(gate.at[m], index, rows), w[2]),
             outv.at[m],
         )
 
@@ -777,12 +762,12 @@
         lax.fori_loop(0, seq // step, after, 0)
 
     def stage_in(m):
-        def part(index, cols):
+        def part(index):
             at = pl.ds(pl.multiple_of(index * rows, rows), rows)
             return (
-                nt(q[m, at, :], w[0, cols, 0:hw])
-                + nt(k[m, at, :], w[0, cols, hw : 2 * hw])
-                + nt(v[m, at, :], w[0, cols, 2 * hw : 3 * hw])
+                nt(q[m, at, :], w[0, :, 0:hw])
+                + nt(k[m, at, :], w[0, :, hw : 2 * hw])
+                + nt(v[m, at, :], w[0, :, 2 * hw : 3 * hw])
             )
 
         sc_i[m].run(part, outv.at[m])
@@ -1066,7 +1051,7 @@
             vm((mbs, rows, width), BF16), vm((mbs, rows, width), BF16),
             vm((heads * QB, hw), BF16),
             *scat,
-            dma((4, n)), dma((4, n)),
+            dma((5, n)), dma((5, n)),
             dma((n + 2,)), dma((n + 2,)),
             dma((16,)),
             dma((mbs, 3)), dma((mbs, 3)), dma((mbs, 3)), dma((mbs, 3)), dma((3,)), dma((3,)),
@@ -1135,7 +1120,7 @@
             *[vm(item.shape, item.dtype) for item in finals[len(results) - turned :]],
             dma((len(results) + 1,)), dma((len(results),)),
         ],
-        compiler_params=pltpu.CompilerParams(vmem_limit_bytes=VMEM_LIMIT // 2),
+        compiler_params=pltpu.CompilerParams(vmem_limit_bytes=VMEM_LIMIT),
     )(tv, *results)
     vecs = [item.reshape(-1) for item in done[len(finals) :]]
     gq, gk, gv, gu, gg, out, g_in = done[:7]

time: 380 us -> 357 us (0.939)
  Pallas kernels: 361 us -> 349 us
  local copies, waits for them, and re-layouts: 16 us -> 5.97 us
    unnamed x22 -> x2, local copies, waits for them, and re-layouts: 13.4 us -> 3.36 us
    pallas_call x1, Pallas kernels: 182 us -> 172 us  [shards(): pl.pallas_call(functools.partial(fwd_kernel, n), name='fwd', out_shape=tu...]
where the time goes in v1:
time: 357 us; the launch traced here: 356 us
  Pallas kernels  349 us (98%)
  local copies, waits for them, and re-layouts  5.97 us (2%)
    pallas_call x1, Pallas kernels, shards(): pl.pallas_call(functools.partial(fwd_kernel, n), name='fwd', out_shape=tu...  172 us
    pallas_call x1, Pallas kernels, shards(): pl.pallas_call(functools.partial(bwd_kernel, n), name='bwd', out_shape=(s...  172 us

profile of v1, /device:TPU:0, one launch (start us, length us, event | category | flops | bytes accessed | tf_op | source)
XLA Modules:
  0.0 356.0 jit_solution(18175150665929145555)
XLA Ops:
  0.6 0.7 pad_bitcast_fusion.2
  1.3 0.7 pad_bitcast_fusion
  2.0 1.3 stack.27.small
  3.3 1.6 copy.29
  4.8 1.8 copy.30
  6.6 172.4 %fwd.1 = (bf16[2,256,1024]{2,1,0:T(8,128)(2,1)}, bf16[4,1024,1024]{2,1,0:T(8,128)(2,1)}, bf16[2,1024,1024]{2,1,0:T(8,128)(2,1)}, bf16[2,1024,256]{2,1,0:T(8,128)...) custom-call(bf16[128,256]{1,0:T(8,128)(2,1)} %wq.1, ...), custom_call_target="tpu_custom_call" | custom-call | tf_op jit(solution)/shard_map/fwd/pallas_call | solution.py:1037
  179.0 172.1 %bwd.1 = (bf16[2,256,1024]{2,1,0:T(8,128)(2,1)}, f32[128,256]{1,0:T(8,128)}, f32[128,256]{1,0:T(8,128)}, f32[128,256]{1,0:T(8,128)}, f32[128,256]{1,0:T(8,128)},...) custom-call(bf16[2,256,1024]{2,1,0:T(8,128)(2,1)} %hid.3, ...), custom_call_target="tpu_custom_call" | custom-call | tf_op jit(solution)/shard_map/bwd/pallas_call | solution.py:1069
  351.1 4.7 %results.1 = (f32[128,256]{1,0:T(8,128)}, f32[128,256]{1,0:T(8,128)}, f32[128,256]{1,0:T(8,128)}, f32[128,1024]{1,0:T(8,128)}, f32[128,1024]{1,0:T(8,128)}, /*in...) custom-call(f32[4,40,128]{2,1,0:T(8,128)} %get-tuple-element.80.i_tv, ...), custom_call_target="tpu_custom_call" | custom-call | tf_op jit(solution)/shard_map/results/pallas_call | solution.py:1111
  (2 shorter events, 0.0 us)

commit v2 on v1

--- a/solution.py
+++ b/solution.py
@@ -196,15 +196,14 @@
     return total
 
 
-def fwd_kernel(
+def layer_kernel(
     n,
     wq, wk, wv, wo, wu, wg, wd, hid, og, small, docs,
-    o_out, o_w, o_x, o_q, o_k, o_v, o_rq, o_rk, o_lrow, o_mixed, o_mid, o_up, o_gate, o_inner,
-    o_attn, o_gmd, o_gm, o_gm0, o_vec, o_acc, o_tab, o_ir,
-    w, x, q, k, v, rq, rk, lcol, mixed, mid, up, gate, inner,
-    attn, midf, mlp, gmd, gm, gm0, vec, acc, tab, ir, sall, docv, ogv, outv, qm, sbuf, rbuf,
-    wsend, wrecv, small_s, small_r, lsem, agx_s, agx_r, agm_s, agm_r, agg_s, agg_r,
-    rsa_s, rsa_r, rsm_s, rsm_r, osem,
+    o_out, o_x, o_mid, o_in, o_gq, o_gk, o_gv, o_go, o_gu, o_gg, o_gd, o_tv,
+    w, x, q, k, v, rqk, lrow, mixed, mid, up, gate, inner, attn, midf, mlp, gmd, vec, acc, tab, ir,
+    docv, ogv, qm, sbuf, rbuf, kt, dk, dv, xrecv, zrecv, vsend, vrecv, tv,
+    wsend, wrecv, small_s, small_r, lsem, agx_s, agx_r, agm_s, agm_r, agg_s, agg_r, aga_s, aga_r,
+    rsa_s, rsa_r, rsm_s, rsm_r, rsb_s, rsb_r, rsi_s, rsi_r, xs, xr, zs, zr, vs, vr, osem,
 ):
     p = Place(n)
     nz = p.nz
@@ -222,6 +221,13 @@
         g, lo, hi = pieces[key]
         return w.at[g, pl.ds(pl.multiple_of(index * shard, shard), shard), pl.ds(lo, hi - lo)]
 
+    ga, gm, back, dqt = x, mid, midf, mlp.at[0]
+    gmix = [inner.at[m, :, pl.ds(0, hw)] for m in range(mbs)]
+    pts, dss = (inner.at[m, pl.ds(0, seq - 128), pl.ds(hw, heads * QB)] for m in range(2))
+    qs, gs = (
+        inner.at[0, pl.ds(i * heads * QB, heads * QB), pl.ds(hw + heads * QB, hw)] for i in range(2)
+    )
+
     local = []
 
     def lcopy(src, dst):
@@ -245,10 +251,13 @@
 
     gx = [Gather(p, x.at[m], agx_s.at[m], agx_r.at[m], rows) for m in range(mbs)]
     gmi = [Gather(p, mid.at[m], agm_s.at[m], agm_r.at[m], rows) for m in range(mbs)]
-    slot = p.t * n + p.d
-    small_own = lcopy(small, sall.at[slot])
+    def seat(t, d):
+        line = pl.ds(pl.multiple_of(t * n + d // 8 * 8, 8), 8)
+        return midf.at[0, line, pl.ds(pl.multiple_of(d % 8 * 128, 128), 128)]
+
+    small_own = lcopy(small, seat(p.t, p.d))
     small_d = [
-        remote(small, sall.at[slot], small_s.at[i], small_r.at[i], dp=peer)
+        remote(small, seat(p.t, p.d), small_s.at[i], small_r.at[i], dp=peer)
         for i, peer in enumerate(p.dpeers)
     ]
     for copy in small_d:
@@ -276,12 +285,12 @@
     xown = [lcopy(hid.at[m], gx[m].at(p.t)) for m in range(mbs)]
     og_in = lcopy(og, ogv)
     for i, peer in enumerate(p.dpeers):
-        src = p.t * n + (p.d + n - (i + 1)) % n
-        remote(sall.at[src], sall.at[src], small_s.at[i], small_r.at[i], dp=peer).wait_recv()
+        src = seat(p.t, (p.d + n - (i + 1)) % n)
+        remote(src, src, small_s.at[i], small_r.at[i], dp=peer).wait_recv()
     small_own.wait()
     small_t = []
     for i, peer in enumerate(p.tpeers):
-        part = sall.at[pl.ds(p.t * n, n)]
+        part = midf.at[0, pl.ds(pl.multiple_of(p.t * n, n), n)]
         copy = remote(part, part, small_s.at[n - 1 + i], small_r.at[n - 1 + i], tensor=peer)
         copy.start()
         small_t.append(copy)
@@ -292,9 +301,6 @@
         for peer in p.zpeers:
             other = peer + 1 - 2 * p.xi
             remote(wat(g, other), wat(g, other), wsend.at[g, 0], wrecv.at[g, other], dp=p.xn).wait_recv()
-        if g:
-            g, _, _ = pieces[g]
-            ocopy(w.at[g], o_w.at[g])
 
     docs_in.wait()
     for m in range(mbs):
@@ -329,7 +335,7 @@
     for g in range(1, len(pieces)):
         wsend_to(g, nz - 1, wat(g, p.d), p.d, p.xn)
     for i, peer in enumerate(p.tpeers):
-        part = sall.at[pl.ds((p.t + 4 - (i + 1)) % 4 * n, n)]
+        part = midf.at[0, pl.ds(pl.multiple_of((p.t + 4 - (i + 1)) % 4 * n, n), n)]
         remote(part, part, small_s.at[n - 1 + i], small_r.at[n - 1 + i], tensor=peer).wait_recv()
     every = 4 * n
 
@@ -337,7 +343,7 @@
         per = count // (lanes // 128)
 
         def item(k):
-            part = sall[k % 4 * n + base + k // 4, row : row + 1, :]
+            part = seat(k % 4, base + k // 4)[row : row + 1, :]
             turn = k % per * (128 // per)
             return pltpu.roll(part, turn, 1) if turn else part
 
@@ -363,16 +369,20 @@
             at = pl.ds(pl.multiple_of(index * rows, rows), rows)
             xb = x[m, at, :]
             cb, sb = turns(tab[m, at, :])
-            for which, (dst, rdst) in enumerate(((q, rq), (k, rk))):
+            scales = []
+            for which, dst in enumerate((q, k)):
                 raw = nn(xb, w[0, :, which * hw : (which + 1) * hw])
                 for half in range(hw // 128):
                     lanes = slice(128 * half, 128 * half + 128)
                     piece = raw[:, lanes]
                     turned = piece * cb + partner(piece) * sb
                     scale = lax.rsqrt(split_sum(turned * turned, ones) + 1e-06)
-                    rdst[m, at, lanes] = scale.astype(BF16)
+                    scales.append(scale)
                     dst[m, at, lanes] = (turned * scale * vec[0:1, lanes]).astype(BF16)
             v[m, at, :] = nn(xb, w[0, :, 2 * hw : 3 * hw]).astype(BF16)
+            for half in range(hw // 128):
+                both = jnp.where(lane_iota(cb.shape) % DH < DH // 2, scales[half], scales[hw // 128 + half])
+                rqk[m, at, 128 * half : 128 * half + 128] = both.astype(BF16)
 
         gx[m].each(work)
 
@@ -404,7 +414,7 @@
                 total = jnp.where(lane == h, part * inv, total)
                 lsum = jnp.where(lane_l == h, inv, lsum)
             mixed[m, at, :] = total.astype(BF16)
-            lcol[m, at, :] = lsum
+            lrow[m, pl.ds(pl.multiple_of(b * 8, 8), 8), :] = jnp.transpose(lsum, (1, 0))[0:8, :]
             return carry
 
         lax.fori_loop(0, seq // QB, body, 0)
@@ -463,7 +473,7 @@
     def stage_down(m):
         sc_m[m].run(lambda index: nt(rows_of(inner.at[m], index, rows), w[3]), mlp.at[m])
 
-    gg = Gather(p, gm0, agg_s, agg_r, rows)
+    gg = [Gather(p, gm.at[m], agg_s.at[m], agg_r.at[m], rows) for m in range(mbs)]
 
     def stage_end(m):
         sc_m[m].finish()
@@ -478,158 +488,25 @@
             zz = h + al * (na - h)
             rz = lax.rsqrt(mean_sq(zz) + 1e-06)
             out = zz * rz
-            outv[m, at, :] = out.astype(BF16)
             cot = ogv[m, at, :].astype(F32)
+            ogv[m, at, :] = out.astype(BF16)
             dz = rz * (cot - out * jnp.mean(cot * out, axis=-1, keepdims=True))
             dn = al * dz
             acc[0:8, :] += fold8(dz * (na - h))
             gmd[m, at, :] = dz - dn
             grad = (ra * (dn - na * jnp.mean(dn * na, axis=-1, keepdims=True))).astype(BF16)
-            gm[m, at, :] = grad
-            if m == 0:
-                gm0[pl.ds(pl.multiple_of(p.t * rows + i * chunk, chunk), chunk), :] = grad
+            gm[m, pl.ds(pl.multiple_of(p.t * rows + i * chunk, chunk), chunk), :] = grad
             return carry
 
         lax.fori_loop(0, rows // chunk, body, 0)
-        if m == 0:
-            gg.start(gg.at(p.t))
-
-    stage_qkv(0)
-    relay(1)
-    attend(0)
-    relay(2)
-    wready(1)
-    stage_o(0)
-    stage_qkv(1)
-    attend(1)
-    stage_mid(0)
-    relay(3)
-    stage_o(1)
-    for m in range(mbs):
-        ocopy(x.at[m], o_x.at[m])
-        ocopy(q.at[m], o_q.at[m])
-        ocopy(k.at[m], o_k.at[m])
-        ocopy(v.at[m], o_v.at[m])
-        ocopy(rq.at[m], o_rq.at[m])
-        ocopy(rk.at[m], o_rk.at[m])
-        ocopy(mixed.at[m], o_mixed.at[m])
-    ocopy(vec, o_vec)
-    ocopy(tab, o_tab)
-    ocopy(ir, o_ir)
-    relay(4)
-    wready(2)
-    wready(3)
-    stage_up(0)
-    stage_mid(1)
-    wready(4)
-    stage_down(0)
-    stage_up(1)
-    stage_down(1)
-    og_in.wait()
-    stage_end(0)
-    ocopy(mid.at[0], o_mid.at[0])
-    ocopy(up.at[0], o_up.at[0])
-    ocopy(gate.at[0], o_gate.at[0])
-    ocopy(inner.at[0], o_inner.at[0])
-    for m in range(mbs):
-        lrow = jnp.transpose(lcol[m], (1, 0))
-        lcol[m, 0:8, 0:128] = lrow[0:8, 0:128]
-        for j in range(1, seq // 128):
-            lcol[m, 8 * j : 8 * j + 8, 0:128] = lrow[0:8, 128 * j : 128 * j + 128]
-        ocopy(lcol.at[m, pl.ds(0, seq // 16)], o_lrow.at[m])
-    ocopy(mid.at[1], o_mid.at[1])
-    ocopy(up.at[1], o_up.at[1])
-    ocopy(gate.at[1], o_gate.at[1])
-    ocopy(inner.at[1], o_inner.at[1])
-    ocopy(attn, o_attn)
-    for step in range(1, 3):
-        gg.wait(step)
-    stage_end(1)
-    ocopy(outv, o_out)
-    ocopy(gmd, o_gmd)
-    ocopy(gm, o_gm)
-    ocopy(acc, o_acc)
-    gg.wait(3)
-    ocopy(gm0, o_gm0)
-    for gather in gx + gmi + [gg]:
-        gather.drain()
-    for copy in sends + small_t + small_d:
-        copy.wait_send()
-    for copy in outs:
-        copy.wait()
-
-
-def bwd_kernel(
-    n,
-    hid, i_w, i_x, i_q, i_k, i_v, i_rq, i_rk, i_lrow, i_mixed, i_mid, i_up, i_gate,
-    i_inner, i_attn, i_gmd, i_gm, i_gm0, i_vec, i_acc, i_tab, i_ir,
-    o_in, o_gq, o_gk, o_gv, o_go, o_gu, o_gg, o_gd, o_tv,
-    w, q, k, v, rq, rk, lrow, mixed, up, gate, inner, attn, gmd, gm, ga, vec, acc,
-    tab, ir, kt, dqt, dk, dv, outv, xrecv, zrecv, vsend, vrecv, tv, sbuf, rbuf,
-    lsem, agg_s, agg_r, aga_s, aga_r, rsm_s, rsm_r, rsi_s, rsi_r, xs, xr, zs, zr, vs, vr, osem,
-):
-    p = Place(n)
-    nz = p.nz
-    mbs, rows, width = hid.shape
-    seq = q.shape[1]
-    hw = q.shape[2]
-    heads = hw // DH
-    hidden = up.shape[2]
-    groups = w.shape[0]
-    shard = width // n
-    gmix = [inner.at[m, :, pl.ds(0, hw)] for m in range(mbs)]
-    pts, dss = (inner.at[m, pl.ds(0, seq - 128), pl.ds(hw, heads * QB)] for m in range(2))
-    qs, gs = (
-        inner.at[0, pl.ds(i * heads * QB, heads * QB), pl.ds(hw + heads * QB, hw)] for i in range(2)
-    )
-
-    local = []
-
-    def lcopy(src, dst):
-        copy = pltpu.make_async_copy(src, dst, lsem.at[len(local)])
-        copy.start()
-        local.append(copy)
-        return copy
-
-    outs = []
-
-    def ocopy(src, dst):
-        copy = pltpu.make_async_copy(src, dst, osem.at[len(outs)])
-        copy.start()
-        outs.append(copy)
-
-    l_gm0 = lcopy(i_gm0, gm.at[0])
-    l_w3 = lcopy(i_w.at[3], w.at[3])
-    l_ug = [[lcopy(i_up.at[m], up.at[m]), lcopy(i_gate.at[m], gate.at[m])] for m in range(mbs)]
-    l_vec = [lcopy(i_vec, vec), lcopy(i_acc, acc)]
-    p.barrier()
-    gg = Gather(p, gm.at[1], agg_s, agg_r, rows)
-    gg.start(i_gm.at[1])
-    l_gm1 = lcopy(i_gm.at[1], gg.at(p.t))
-    l_w12 = [lcopy(i_w.at[1], w.at[1]), lcopy(i_w.at[2], w.at[2])]
-    l_inner = [lcopy(i_inner.at[m], inner.at[m]) for m in range(mbs)]
-    l_rows = [lcopy(i_attn, attn), lcopy(i_gmd, gmd)]
-    l_w0 = lcopy(i_w.at[0], w.at[0])
-    l_att = [
-        [
-            lcopy(src.at[m], dst.at[m])
-            for src, dst in ((i_q, q), (i_k, k), (i_v, v), (i_rq, rq), (i_rk, rk), (i_lrow, lrow), (i_mixed, mixed))
-        ]
-        for m in range(mbs)
-    ]
-    l_tab = [lcopy(i_tab, tab), lcopy(i_ir, ir)]
+        gg[m].start(gg[m].at(p.t))
 
     gga = [Gather(p, ga.at[m], aga_s.at[m], aga_r.at[m], rows) for m in range(mbs)]
-    l_hid = [lcopy(hid.at[m], gga[m].at(p.t)) for m in range(mbs)]
-    sc_m = [Scatter(p, sbuf.at[m], rbuf.at[m], rsm_s.at[m], rsm_r.at[m]) for m in range(mbs)]
+    sc_b = [Scatter(p, sbuf.at[m], rbuf.at[m], rsb_s.at[m], rsb_r.at[m]) for m in range(mbs)]
     sc_i = [Scatter(p, sbuf.at[m], rbuf.at[m], rsi_s.at[m], rsi_r.at[m]) for m in range(mbs)]
     cols = 256
-    chunk = 32
 
     def stage_inner(m):
-        if m == 1:
-            l_gm1.wait()
-
         def work(index):
             at = pl.ds(pl.multiple_of(index * rows, rows), rows)
 
@@ -652,23 +529,23 @@
 
             lax.fori_loop(0, hidden // WIDE, body, 0)
 
-        blocks(p, work, gg.wait if m == 1 else None)
+        gg[m].each(work)
 
     def stage_back(m):
-        sc_m[m].run(
+        sc_b[m].run(
             lambda index: nt(rows_of(up.at[m], index, rows), w[1])
             + nt(rows_of(gate.at[m], index, rows), w[2]),
-            outv.at[m],
+            back.at[m],
         )
 
     def stage_attn(m):
-        sc_m[m].finish()
+        sc_b[m].finish()
         base = p.t * rows
 
         def body(i, carry):
             at = pl.ds(pl.multiple_of(i * chunk, chunk), chunk)
             own = pl.ds(pl.multiple_of(base + i * chunk, chunk), chunk)
-            part = outv[m, at, :] + rbuf[m, 1, at, :].astype(F32)
+            part = back[m, at, :] + rbuf[m, 1, at, :].astype(F32)
             cot = gmd[m, at, :] + part + rbuf[m, 2, at, :].astype(F32)
             a = attn[m, at, :]
             h = ga[m, own, :].astype(F32)
@@ -695,11 +572,7 @@
 
         gga[m].each(work)
 
-    win = seq - 128
-    c_exp = math.sqrt(DH) * LOG2E
-    ones = head_ones()
-
-    def attend(m):
+    def attend_back(m):
         kt[...] = jnp.transpose(k[m], (1, 0))
         dk[...] = jnp.zeros_like(dk)
         dv[...] = jnp.zeros_like(dv)
@@ -744,7 +617,6 @@
             v[m, at, :] = dv[at, :].astype(BF16)
             for which in range(2):
                 src = (q, k)[which]
-                rsc = (rq, rk)[which]
                 for half in range(hw // 128):
                     lanes = slice(128 * half, 128 * half + 128)
                     if which == 0:
@@ -755,7 +627,10 @@
                     unit = src[m, at, lanes].astype(F32) / gain
                     acc[32:40, lanes] += fold8(grad * unit)
                     dn = grad * gain
-                    dy = rsc[m, at, lanes].astype(F32) * (dn - unit * split_sum(dn * unit, ones))
+                    both = rqk[m, at, lanes].astype(F32)
+                    first = lane_iota(both.shape) % DH < DH // 2
+                    rsc = jnp.where(first, both, partner(both)) if which == 0 else jnp.where(first, partner(both), both)
+                    dy = rsc * (dn - unit * split_sum(dn * unit, ones))
                     src[m, at, lanes] = (dy * cb - partner(dy) * sb).astype(BF16)
             return carry
 
@@ -770,14 +645,14 @@
                 + nt(v[m, at, :], w[0, :, 2 * hw : 3 * hw])
             )
 
-        sc_i[m].run(part, outv.at[m])
+        sc_i[m].run(part, back.at[m])
 
     def stage_out(m):
         sc_i[m].finish()
 
         def body(i, carry):
             at = pl.ds(pl.multiple_of(i * chunk, chunk), chunk)
-            part = outv[m, at, :] + rbuf[m, 1, at, :].astype(F32)
+            part = back[m, at, :] + rbuf[m, 1, at, :].astype(F32)
             total = gmd[m, at, :] + part + rbuf[m, 2, at, :].astype(F32)
             sbuf[m, 0, at, :] = total.astype(BF16)
             return carry
@@ -785,7 +660,7 @@
         lax.fori_loop(0, rows // chunk, body, 0)
         ocopy(sbuf.at[m, 0], o_in.at[m])
 
-    pieces = {
+    gpieces = {
         3: (w.at[3], 3, 0, width),
         1: (w.at[1], 1, 0, width),
         2: (w.at[2], 2, 0, width),
@@ -794,7 +669,7 @@
     }
 
     def weight_grad(key, left, rights):
-        into = pieces[key][0]
+        into = gpieces[key][0]
 
         def body(c, carry):
             lanes = pl.ds(pl.multiple_of(c * cols, cols), cols)
@@ -808,11 +683,11 @@
         lax.fori_loop(0, width // cols, body, 0)
 
     def wrow(key, index):
-        ref, _, lo, hi = pieces[key]
+        ref, _, lo, hi = gpieces[key]
         return ref.at[pl.ds(pl.multiple_of(index * shard, shard), shard), pl.ds(lo, hi - lo)]
 
     def held(buf, key, index):
-        _, g, lo, hi = pieces[key]
+        _, g, lo, hi = gpieces[key]
         return buf.at[g, index, :, pl.ds(lo, hi - lo)]
 
     gsends = []
@@ -841,7 +716,7 @@
             gsends.append(copy)
 
     def rs_end(key):
-        _, g, lo, hi = pieces[key]
+        _, g, lo, hi = gpieces[key]
         got, _ = rs_arrive(key, 0)
         total = got[...].astype(F32) + wrow(key, p.d)[...].astype(F32)
         for kk in range(1, nz):
@@ -857,33 +732,63 @@
         else:
             ocopy(fin, (o_gu, o_gg, o_gd)[g - 1])
 
-    for copy in l_vec + [l_gm0, l_w3] + l_ug[0]:
-        copy.wait()
+    stage_qkv(0)
+    kept_x = [lcopy(x.at[0], o_x.at[0])]
+    relay(1)
+    attend(0)
+    relay(2)
+    wready(1)
+    stage_o(0)
+    stage_qkv(1)
+    kept_x.append(lcopy(x.at[1], o_x.at[1]))
+    attend(1)
+    for copy in small_t + small_d:
+        copy.wait_send()
+    stage_mid(0)
+    relay(3)
+    stage_o(1)
+    relay(4)
+    wready(2)
+    wready(3)
+    stage_up(0)
+    kept_mid = [lcopy(mid.at[0], o_mid.at[0])]
+    stage_mid(1)
+    wready(4)
+    gmi[0].drain()
+    kept_mid[0].wait()
+    stage_down(0)
+    stage_up(1)
+    kept_mid.append(lcopy(mid.at[1], o_mid.at[1]))
+    gmi[1].drain()
+    kept_mid[1].wait()
+    stage_down(1)
+    og_in.wait()
+    stage_end(0)
+    for m in range(mbs):
+        gx[m].drain()
+        kept_x[m].wait()
+    for copy in sends:
+        copy.wait_send()
+    stage_end(1)
+    ocopy(ogv, o_out)
     stage_inner(0)
-    for copy in l_w12:
-        copy.wait()
     stage_back(0)
-    for copy in l_ug[1]:
-        copy.wait()
     stage_inner(1)
-    for copy in l_inner + l_rows + l_hid:
-        copy.wait()
     weight_grad(3, gm, [(0, hidden, inner)])
     rs_start(3)
-    gg.drain()
-    l_mid = [lcopy(i_mid.at[m], gm.at[m]) for m in range(mbs)]
+    for gather in gg:
+        gather.drain()
+    l_mid = [lcopy(o_mid.at[m], gm.at[m]) for m in range(mbs)]
     stage_attn(0)
     stage_back(1)
     for copy in l_mid:
         copy.wait()
     weight_grad(1, gm, [(0, hidden, up)])
     rs_start(1)
-    l_x = [lcopy(i_x.at[m], up.at[m]) for m in range(mbs)]
-    for copy in [l_w0] + l_tab + l_att[0] + l_att[1]:
-        copy.wait()
+    l_x = [lcopy(o_x.at[m], up.at[m]) for m in range(mbs)]
     stage_mixed(0)
     rs_mid(3)
-    attend(0)
+    attend_back(0)
     stage_attn(1)
     stage_in(0)
     weight_grad(2, gm, [(0, hidden, gate)])
@@ -892,7 +797,7 @@
     stage_mixed(1)
     weight_grad(4, ga, [(3 * hw, 4 * hw, mixed)])
     rs_start(4)
-    attend(1)
+    attend_back(1)
     rs_mid(2)
 
     per = width // 128
@@ -1004,103 +909,48 @@
     def sds(shape, dtype):
         return jax.ShapeDtypeStruct(shape, dtype)
 
-    res_shapes = dict(
-        out=((mbs, rows, width), BF16),
-        w=((4, width, width), BF16),
-        x=((mbs, seq, width), BF16),
-        q=((mbs, seq, hw), BF16),
-        k=((mbs, seq, hw), BF16),
-        v=((mbs, seq, hw), BF16),
-        rq=((mbs, seq, hw), BF16),
-        rk=((mbs, seq, hw), BF16),
-        lrow=((mbs, seq // 16, 128), F32),
-        mixed=((mbs, seq, hw), BF16),
-        mid=((mbs, seq, width), BF16),
-        up=((mbs, seq, hidden), BF16),
-        gate=((mbs, seq, hidden), BF16),
-        inner=((mbs, seq, hidden), BF16),
-        attn=((mbs, rows, width), F32),
-        gmd=((mbs, rows, width), F32),
-        gm=((mbs, rows, width), BF16),
-        gm0=((seq, width), BF16),
-        vec=((8, width), F32),
-        acc=((40, width), F32),
-        tab=((mbs, seq, 128), F32),
-        ir=((mbs, 8, seq), F32),
-    )
-    r = {key: sds(*val) for key, val in res_shapes.items()}
-    s = {key: vm(*val) for key, val in res_shapes.items()}
     nvec = 5 * (width // 128)
-    own32 = vm((mbs, rows, width), F32)
-    scat = [vm((mbs, 3, rows, width), BF16), vm((mbs, 3, rows, width), BF16)]
+    rows32 = vm((mbs, rows, width), F32)
+    rows16 = vm((mbs, rows, width), BF16)
+    full = vm((mbs, seq, width), BF16)
+    wide = vm((mbs, seq, hidden), BF16)
+    slim = vm((mbs, seq, hw), BF16)
+    scat = vm((mbs, 3, rows, width), BF16)
+    pair = dma((mbs, 3))
     heads = hw // DH
-    res = pl.pallas_call(
-        functools.partial(fwd_kernel, n),
-        name="fwd",
-        out_shape=tuple(r.values()),
+    gshape = sds((shard, hw), F32)
+    fshape = sds((shard, hidden), F32)
+    g_out, _, _, g_in, gq, gk, gv, go, gu, gg, gd, tv = pl.pallas_call(
+        functools.partial(layer_kernel, n),
+        name="layer",
+        out_shape=(
+            sds((mbs, rows, width), BF16), sds((mbs, seq, width), BF16), sds((mbs, seq, width), BF16),
+            sds((mbs, rows, width), BF16), gshape, gshape, gshape, gshape, fshape, fshape, fshape,
+            sds((4, nvec, 128), F32),
+        ),
         in_specs=[any_] * 11,
-        out_specs=tuple([any_] * len(r)),
+        out_specs=(any_,) * 12,
         scratch_shapes=[
-            s["w"], s["x"], s["q"], s["k"], s["v"], s["rq"], s["rk"],
-            vm((mbs, seq, 128), F32),
-            s["mixed"], s["mid"], s["up"], s["gate"], s["inner"],
-            s["attn"], own32, own32, s["gmd"], s["gm"], s["gm0"], s["vec"], s["acc"],
-            s["tab"], s["ir"],
-            vm((4 * n, 8, 128), F32),
-            vm((mbs, 1, seq), jnp.int32),
-            vm((mbs, rows, width), BF16), vm((mbs, rows, width), BF16),
-            vm((heads * QB, hw), BF16),
-            *scat,
-            dma((5, n)), dma((5, n)),
-            dma((n + 2,)), dma((n + 2,)),
-            dma((16,)),
-            dma((mbs, 3)), dma((mbs, 3)), dma((mbs, 3)), dma((mbs, 3)), dma((3,)), dma((3,)),
-            dma((mbs, 3)), dma((mbs, 3)), dma((mbs, 3)), dma((mbs, 3)),
-            dma((40,)),
+            vm((4, width, width), BF16), full, slim, slim, slim, slim,
+            vm((mbs, seq // 16, 128), F32), slim, full, wide, wide, wide,
+            rows32, rows32, rows32, rows32, vm((8, width), F32), vm((40, width), F32),
+            vm((mbs, seq, 128), F32), vm((mbs, 8, seq), F32),
+            vm((mbs, 1, seq), jnp.int32), rows16, vm((heads * QB, hw), BF16),
+            scat, scat,
+            vm((hw, seq), BF16), vm((seq, hw), F32), vm((seq, hw), F32),
+            vm((4, nz, shard, width), BF16), vm((4, nz - 1, shard, width), BF16),
+            vm((nvec, 128), F32), vm((n - 1, nvec, 128), F32), vm((4, nvec, 128), F32),
+            dma((5, n)), dma((5, n)), dma((n + 2,)), dma((n + 2,)), dma((24,)),
+            pair, pair, pair, pair, pair, pair, pair, pair,
+            pair, pair, pair, pair, pair, pair, pair, pair,
+            dma((5, nz)), dma((5, nz)), dma((5, nz - 1)), dma((5, nz - 1)),
+            dma((n + 2,)), dma((n + 2,)), dma((16,)),
         ],
         compiler_params=pltpu.CompilerParams(
             collective_id=0, has_side_effects=True, vmem_limit_bytes=VMEM_LIMIT
         ),
     )(w_query, w_key, w_value, w_output.T, w_up, w_gate, w_down.T, hidden_in, out_grad, small, doc_ids)
-    r = dict(zip(r, res))
-
-    gshape = sds((shard, hw), F32)
-    fshape = sds((shard, hidden), F32)
-    grads = pl.pallas_call(
-        functools.partial(bwd_kernel, n),
-        name="bwd",
-        out_shape=(
-            sds((mbs, rows, width), BF16), gshape, gshape, gshape, gshape, fshape, fshape, fshape,
-            sds((4, nvec, 128), F32),
-        ),
-        in_specs=[any_] * 22,
-        out_specs=tuple([any_] * 9),
-        scratch_shapes=[
-            s["w"], s["q"], s["k"], s["v"], s["rq"], s["rk"], s["lrow"], s["mixed"],
-            s["up"], s["gate"], s["inner"], s["attn"], s["gmd"],
-            s["x"], s["x"], s["vec"], s["acc"],
-            s["tab"], s["ir"],
-            vm((hw, seq), BF16), vm((hw, seq), F32), vm((seq, hw), F32), vm((seq, hw), F32),
-            own32,
-            vm((4, nz, shard, width), BF16), vm((4, nz - 1, shard, width), BF16),
-            vm((nvec, 128), F32), vm((n - 1, nvec, 128), F32), vm((4, nvec, 128), F32),
-            *scat,
-            dma((48,)), dma((3,)), dma((3,)), dma((mbs, 3)), dma((mbs, 3)),
-            dma((mbs, 3)), dma((mbs, 3)), dma((mbs, 3)), dma((mbs, 3)),
-            dma((5, nz)), dma((5, nz)), dma((5, nz - 1)), dma((5, nz - 1)),
-            dma((n + 2,)), dma((n + 2,)),
-            dma((16,)),
-        ],
-        compiler_params=pltpu.CompilerParams(
-            collective_id=1, has_side_effects=True, vmem_limit_bytes=VMEM_LIMIT
-        ),
-    )(
-        hidden_in, r["w"], r["x"], r["q"], r["k"], r["v"], r["rq"], r["rk"], r["lrow"],
-        r["mixed"], r["mid"], r["up"], r["gate"], r["inner"], r["attn"], r["gmd"], r["gm"], r["gm0"],
-        r["vec"], r["acc"], r["tab"], r["ir"],
-    )
-    g_in, gq, gk, gv, go, gu, gg, gd, tv = grads
-    results = [gq, gk, gv, gu, gg, r["out"], g_in, go, gd]
+    results = [gq, gk, gv, gu, gg, g_out, g_in, go, gd]
     turned = 2 if shard % 128 == 0 else 0
     if not turned:
         results = results[:-2]

time: 357 us -> 347 us (0.972)
  the two profiles are of different devices: /device:TPU:0 before, /device:TPU:24 now
where the time goes in v2:
time: 347 us
  Pallas kernels  340 us (98%)
  local copies, waits for them, and re-layouts  5.97 us (2%)
    pallas_call x1, Pallas kernels, shards(): pl.pallas_call(functools.partial(layer_kernel, n), name='layer', out_shap...  335 us

profile of v2, /device:TPU:24, one launch (start us, length us, event | category | flops | bytes accessed | tf_op | source)
XLA Modules:
  0.0 346.7 jit_solution(4698928424980172091)
XLA Ops:
  0.6 0.7 pad_bitcast_fusion.2
  1.3 0.7 pad_bitcast_fusion
  2.0 1.3 stack.27.small
  3.3 1.6 copy.29
  4.8 1.8 copy.30
  6.6 335.2 %layer.1 = (bf16[2,256,1024]{2,1,0:T(8,128)(2,1)}, bf16[2,1024,1024]{2,1,0:T(8,128)(2,1)}, bf16[2,1024,1024]{2,1,0:T(8,128)(2,1)}, bf16[2,256,1024]{2,1,0:T(8,12...) custom-call(bf16[128,256]{1,0:T(8,128)(2,1)} %wq.1, ...), custom_call_target="tpu_custom_call" | custom-call | tf_op jit(solution)/shard_map/layer/pallas_call | solution.py:923
  341.9 4.7 %results.1 = (f32[128,256]{1,0:T(8,128)}, f32[128,256]{1,0:T(8,128)}, f32[128,256]{1,0:T(8,128)}, f32[128,1024]{1,0:T(8,128)}, f32[128,1024]{1,0:T(8,128)}, /*in...) custom-call(f32[4,40,128]{2,1,0:T(8,128)} %get-tuple-element.38.i_tv, ...), custom_call_target="tpu_custom_call" | custom-call | tf_op jit(solution)/shard_map/results/pallas_call | solution.py:961
  (2 shorter events, 0.0 us)
